TPU v7x, 32 devices: a whole 2x2x4 slice. The times are simulated.
32 devices in a mesh: groups: 2 (over y), space: 4 (over z), tm: 2 (over x), chan: 2 (over core).
Axes of the slice: x: 2, y: 2, z: 4, core: 2. Of those that a mesh axis runs over, the one named last changes fastest.
Arguments:
- latent: bfloat16 [4, 16, 1024], P(('groups', 'tm'), 'space'), parts along dimension 0, may hold values from -12 to 12
- in_weight: bfloat16 [432, 384], P(None, 'chan'), may hold values from -1.5 to 1.5
- in_bias: float32 [384], P('chan'), may hold values from -1.5 to 1.5
- first_gain: float32 [384], replicated, may hold values from 0.25 to 1.75
- first_weight: bfloat16 [9, 1152, 384], P(None, None, 'chan'), may hold values from -0.0625 to 0.0625
- first_bias: float32 [384], P('chan'), may hold values from -1.5 to 1.5
- second_gain: float32 [384], replicated, may hold values from 0.25 to 1.75
- second_weight: bfloat16 [9, 1152, 384], P(None, None, 'chan'), may hold values from -0.0625 to 0.0625
- second_bias: float32 [384], P('chan'), may hold values from -1.5 to 1.5
- up_weight: bfloat16 [3, 1152, 192], P(None, None, 'chan'), may hold values from -0.109375 to 0.109375
- up_bias: float32 [192], P('chan'), may hold values from -1.5 to 1.5
Outputs:
- decoded: bfloat16 [8, 16, 192, 128], P(('groups', 'tm'), 'space', 'chan'), parts along dimension 0
There are 2 independent parts, one for each index of `groups`. A program takes and returns all parts, laid end to end along the dimension named above; an argument that names none is the same for every part. Nothing has to cross between parts.
All inputs are finite; a program needn't handle non-finite values.
Results may differ from a plain program's by a relative error of at most 0.0058.
Values may be sent and summed in bfloat16 or wider, within the bound.
No kernel may reach another device: no remote copies, remote signals or barrier semaphores. Data moves between devices by JAX's collectives and lax.ppermute only.
A program may use at most 64 MiB of HBM per device.

v0:
```python
import jax
import jax.numpy as jnp
from jax import lax
from jax.sharding import PartitionSpec as P

ZC = 16
C = 384
FS = 2
LW = 64


epsilon = 1e-06


def passed_along(array, axis, by):
    count = lax.axis_size(axis)
    pairs = [(i, i + by) for i in range(count) if 0 <= i + by < count]
    return lax.ppermute(array, axis, pairs)


def padded_2(block, sides, width):
    for axis, dim in sides:
        count = lax.axis_size(axis)
        forward = [(i, i + 1) for i in range(count - 1)]
        backward = [(target, source) for source, target in forward]
        low = lax.ppermute(
            lax.slice_in_dim(block, block.shape[dim] - width, None, axis=dim), axis, forward
        )
        high = lax.ppermute(lax.slice_in_dim(block, 0, width, axis=dim), axis, backward)
        block = jnp.concatenate([low, block, high], axis=dim)
    return block


def width_taps(tap_slab):
    col_count = tap_slab.shape[-2] - 2
    return jnp.concatenate(
        [
            tap_slab[..., 0:col_count, :],
            tap_slab[..., 1 : col_count + 1, :],
            tap_slab[..., 2 : col_count + 2, :],
        ],
        axis=-1,
    )


def conv_taps(extended, weight, tap_depth):
    frame_count = extended.shape[0] - tap_depth + 1
    row_count = extended.shape[1] - 2
    out_chan = weight.shape[-1]
    padded = jnp.pad(extended, ((0, 0), (0, 0), (1, 1), (0, 0)))
    col_count = padded.shape[2] - 2
    running = jnp.zeros((frame_count * row_count * col_count, out_chan), jnp.float32)
    for tap_index in range(tap_depth * 3):
        depth_at = tap_index // 3
        row_at = tap_index % 3
        tap_slab = padded[depth_at : depth_at + frame_count, row_at : row_at + row_count]
        tap_cols = width_taps(tap_slab).reshape(frame_count * row_count * col_count, -1)
        running = running + jnp.dot(
            tap_cols, weight[tap_index].reshape(-1, out_chan), preferred_element_type=jnp.float32
        )
    return running


def activate(values, gain_vec, squares):
    factor = lax.rsqrt(squares[..., None] / C + epsilon)
    return jax.nn.silu(values * factor * gain_vec).astype(jnp.bfloat16)


def upsample(extended):
    taller = jnp.repeat(extended, 2, axis=1)[:, 1:-1]
    return jnp.repeat(taller, 2, axis=2)


def join_chan(own_part):
    return lax.all_gather(own_part, "chan", axis=3, tiled=True)


def extend_all(all_chan, temporal):
    if temporal:
        earlier = passed_along(all_chan, "tm", 1)
        all_chan = jnp.concatenate([earlier, all_chan], axis=0)
    return padded_2(all_chan, (("space", 1),), 1)


def shards(
    latent,
    in_weight,
    in_bias,
    first_gain,
    first_weight,
    first_bias,
    second_gain,
    second_weight,
    second_bias,
    up_weight,
    up_bias,
):
    space_count = lax.axis_size("space")
    space_index = lax.axis_index("space")
    half_chan = first_weight.shape[-1]
    row_count = latent.shape[1] // FS
    gathered = lax.all_gather(latent, "space", axis=1, tiled=True)
    section_rows = gathered.reshape(FS, row_count * space_count, LW * ZC)
    section_rows = jnp.pad(section_rows, ((0, 0), (1, 1), (0, 0)))
    local_rows = lax.dynamic_slice_in_dim(section_rows, space_index * row_count, row_count + 2, 1)
    frames_here = FS
    cols_here = LW
    earlier = passed_along(local_rows, "tm", 1)
    stacked = jnp.concatenate([earlier, local_rows], axis=0).reshape(FS + 2, row_count + 2, LW, ZC)
    padded = jnp.pad(stacked, ((0, 0), (0, 0), (1, 1), (0, 0)))
    voxels = frames_here * row_count * cols_here
    pieces = []
    for depth_at in range(3):
        for row_at in range(3):
            for col_at in range(3):
                pieces.append(
                    padded[
                        depth_at : depth_at + frames_here,
                        row_at : row_at + row_count,
                        col_at : col_at + cols_here,
                    ]
                )
    tap_cols = jnp.concatenate(pieces, axis=-1).reshape(voxels, 27 * ZC)
    first_out = (jnp.dot(tap_cols, in_weight, preferred_element_type=jnp.float32) + in_bias).astype(
        jnp.bfloat16
    )
    first_out = first_out.reshape(frames_here, row_count, cols_here, half_chan)
    conv_one = first_weight.reshape(9, 3, C, half_chan)
    conv_two = second_weight.reshape(9, 3, C, half_chan)
    conv_up = up_weight.reshape(3, 3, C, up_weight.shape[-1])
    values = join_chan(first_out).astype(jnp.float32)
    first_act = activate(values, first_gain, jnp.sum(values * values, axis=-1))
    product = conv_taps(extend_all(first_act, True), conv_one, 3)
    second_out = (
        (product + first_bias)
        .astype(jnp.bfloat16)
        .reshape(frames_here, row_count, cols_here, half_chan)
    )
    values = join_chan(second_out).astype(jnp.float32)
    second_act = activate(values, second_gain, jnp.sum(values * values, axis=-1))
    product = conv_taps(extend_all(second_act, True), conv_two, 3)
    block_out = (
        first_out.astype(jnp.float32).reshape(voxels, half_chan) + product + second_bias
    ).astype(jnp.bfloat16)
    block_out = block_out.reshape(frames_here, row_count, cols_here, half_chan)
    upsampled = upsample(extend_all(join_chan(block_out), False))
    product = conv_taps(upsampled, conv_up, 1)
    output = (
        (product + up_bias)
        .astype(jnp.bfloat16)
        .reshape(frames_here, 2 * row_count, 2 * cols_here, -1)
    )
    return jnp.transpose(output, (0, 1, 3, 2))


def solution(mesh):
    placed = (
        P(("groups", "tm"), "space", None),
        P(None, "chan"),
        P("chan"),
        P(),
        P(None, None, "chan"),
        P("chan"),
        P(),
        P(None, None, "chan"),
        P("chan"),
        P(None, None, "chan"),
        P("chan"),
    )
    return jax.shard_map(
        shards,
        mesh=mesh,
        in_specs=placed,
        out_specs=P(("groups", "tm"), "space", "chan", None),
        check_vma=False,
    )
```

profile of v0, /device:TPU:0, one launch (start us, length us, event | category | flops | bytes accessed | tf_op | source)
XLA Modules:
  0.0 114.0 jit_solution(12747403123316709483)
XLA Ops:
  0.8 14.9 %all_gather.12 = bf16[1,16,1024]{2,0,1:T(2,128)(2,1)S(1)} all-gather(bf16[1,4,1024]{2,0,1:T(2,128)(2,1)S(1)} %copy.29), channel_id=1, replica_groups=mesh['groups'=2,'space'=4,'tm'=2,'chan'=2] {'space'}, dimensions={1}, use_global_device_ids=true | all-gather | bytes 40960 | tf_op jit(solution)/shard_map/all_gather | solution.py:102
  15.7 3.4 %collective-permute-start = (bf16[2,4,1024]{2,1,0:T(4,128)(2,1)S(1)}, bf16[2,4,1024]{2,1,0:T(4,128)(2,1)S(1)}, u32[]{:S(2)}, u32[]{:S(2)}) collective-permute-start(bf16[2,4,1024]{2,1,0:T(4,128)(2,1)S(1)} %pad_dynamic-slice_fusion), channel_id=1, source_target_pairs={{0,2},{1,3},{4,6},{5,7},{8,10},{9,11},{12,14},{13,15},{16,18},{17,... | collective-permute-start | bytes 49160 | tf_op jit(solution)/shard_map/ppermute | solution.py:18
  19.1 1.4 %collective-permute-done = bf16[2,4,1024]{2,1,0:T(4,128)(2,1)S(1)} collective-permute-done((bf16[2,4,1024]{2,1,0:T(4,128)(2,1)S(1)}, bf16[2,4,1024]{2,1,0:T(4,128)(2,1)S(1)}, u32[]{:S(2)}, u32[]{:S(2)}) %collective-permute-start) | collective-permute-done | bytes 16416 | tf_op jit(solution)/shard_map/ppermute | solution.py:18
  22.7 2.1 %all_gather.13 = bf16[2,2,64,384]{2,1,0,3:T(2,128)(2,1)S(1)} all-gather(bf16[2,2,64,192]{2,1,0,3:T(2,128)(2,1)S(1)} %copy.31), channel_id=1, replica_groups=mesh['groups'=2,'space'=4,'tm'=2,'chan'=2] {'chan'}, dimensions={3}, use_global_device_ids=true | all-gather | bytes 294912 | tf_op jit(solution)/shard_map/all_gather | solution.py:75
  25.7 4.2 %collective-permute-start.1 = (bf16[2,2,64,384]{3,2,1,0:T(8,128)(2,1)S(1)}, bf16[2,2,64,384]{3,2,1,0:T(8,128)(2,1)S(1)}, u32[]{:S(2)}, u32[]{:S(2)}) collective-permute-start(bf16[2,2,64,384]{3,2,1,0:T(8,128)(2,1)S(1)} %fusion.68), channel_id=1, source_target_pairs={{0,2},{1,3},{4,6},{5,7},{8,10},{9,11},{12,14},{13,15},{16,18},{17,... | collective-permute-start | bytes 589832 | tf_op jit(solution)/shard_map/ppermute | solution.py:18
  29.9 4.4 %collective-permute-done.1 = bf16[2,2,64,384]{3,2,1,0:T(8,128)(2,1)S(1)} collective-permute-done((bf16[2,2,64,384]{3,2,1,0:T(8,128)(2,1)S(1)}, bf16[2,2,64,384]{3,2,1,0:T(8,128)(2,1)S(1)}, u32[]{:S(2)}, u32[]{:S(2)}) %collective-permute-start.1) | collective-permute-done | bytes 196640 | tf_op jit(solution)/shard_map/ppermute | solution.py:18
  34.4 3.6 %collective-permute-start.2 = (bf16[4,1,64,384]{3,2,1,0:T(8,128)(2,1)S(1)}, bf16[4,1,64,384]{3,2,1,0:T(8,128)(2,1)S(1)}, u32[]{:S(2)}, u32[]{:S(2)}) collective-permute-start(bf16[4,1,64,384]{3,2,1,0:T(8,128)(2,1)S(1)} %get-tuple-element.70), channel_id=1, source_target_pairs={{0,4},{4,8},{8,12},{1,5},{5,9},{9,13},{2,6},{6,10},{10,14},{3,7},{... | collective-permute-start | bytes 589832 | tf_op jit(solution)/shard_map/ppermute | solution.py:26
  39.3 2.3 %collective-permute-done.2 = bf16[4,1,64,384]{3,2,1,0:T(8,128)(2,1)S(1)} collective-permute-done((bf16[4,1,64,384]{3,2,1,0:T(8,128)(2,1)S(1)}, bf16[4,1,64,384]{3,2,1,0:T(8,128)(2,1)S(1)}, u32[]{:S(2)}, u32[]{:S(2)}) %collective-permute-start.2) | collective-permute-done | bytes 196640 | tf_op jit(solution)/shard_map/ppermute | solution.py:26
  41.5 4.1 %collective-permute-done.3 = bf16[4,1,64,384]{3,2,1,0:T(8,128)(2,1)S(1)} collective-permute-done((bf16[4,1,64,384]{3,2,1,0:T(8,128)(2,1)S(1)}, bf16[4,1,64,384]{3,2,1,0:T(8,128)(2,1)S(1)}, u32[]{:S(2)}, u32[]{:S(2)}) %collective-permute-start.3) | collective-permute-done | bytes 196640 | tf_op jit(solution)/shard_map/ppermute | solution.py:29
  47.0 1.8 %copy-done.1 = bf16[9,1152,192]{1,2,0:T(8,128)(2,1)S(1)} copy-done((bf16[9,1152,192]{1,2,0:T(8,128)(2,1)S(1)}, bf16[9,1152,192]{1,2,0:T(8,128)(2,1)}, u32[]{:S(2)}) %copy-start.1) | copy-done | bytes 3981336
  53.1 2.1 %all_gather.14 = bf16[2,2,64,384]{2,1,0,3:T(2,128)(2,1)S(1)} all-gather(bf16[2,2,64,192]{2,1,0,3:T(2,128)(2,1)S(1)} %copy.34), channel_id=1, replica_groups=mesh['groups'=2,'space'=4,'tm'=2,'chan'=2] {'chan'}, dimensions={3}, use_global_device_ids=true | all-gather | bytes 294912 | tf_op jit(solution)/shard_map/all_gather | solution.py:75
  56.2 4.4 %collective-permute-start.4 = (bf16[2,2,64,384]{3,2,1,0:T(8,128)(2,1)S(1)}, bf16[2,2,64,384]{3,2,1,0:T(8,128)(2,1)S(1)}, u32[]{:S(2)}, u32[]{:S(2)}) collective-permute-start(bf16[2,2,64,384]{3,2,1,0:T(8,128)(2,1)S(1)} %fusion.76), channel_id=1, source_target_pairs={{0,2},{1,3},{4,6},{5,7},{8,10},{9,11},{12,14},{13,15},{16,18},{17,... | collective-permute-start | bytes 589832 | tf_op jit(solution)/shard_map/ppermute | solution.py:18
  60.6 4.4 %collective-permute-done.4 = bf16[2,2,64,384]{3,2,1,0:T(8,128)(2,1)S(1)} collective-permute-done((bf16[2,2,64,384]{3,2,1,0:T(8,128)(2,1)S(1)}, bf16[2,2,64,384]{3,2,1,0:T(8,128)(2,1)S(1)}, u32[]{:S(2)}, u32[]{:S(2)}) %collective-permute-start.4) | collective-permute-done | bytes 196640 | tf_op jit(solution)/shard_map/ppermute | solution.py:18
  65.1 3.1 %collective-permute-start.5 = (bf16[4,1,64,384]{3,2,1,0:T(8,128)(2,1)S(1)}, bf16[4,1,64,384]{3,2,1,0:T(8,128)(2,1)S(1)}, u32[]{:S(2)}, u32[]{:S(2)}) collective-permute-start(bf16[4,1,64,384]{3,2,1,0:T(8,128)(2,1)S(1)} %get-tuple-element.66), channel_id=1, source_target_pairs={{0,4},{4,8},{8,12},{1,5},{5,9},{9,13},{2,6},{6,10},{10,14},{3,7},{... | collective-permute-start | bytes 589832 | tf_op jit(solution)/shard_map/ppermute | solution.py:26
  69.5 2.3 %collective-permute-done.5 = bf16[4,1,64,384]{3,2,1,0:T(8,128)(2,1)S(1)} collective-permute-done((bf16[4,1,64,384]{3,2,1,0:T(8,128)(2,1)S(1)}, bf16[4,1,64,384]{3,2,1,0:T(8,128)(2,1)S(1)}, u32[]{:S(2)}, u32[]{:S(2)}) %collective-permute-start.5) | collective-permute-done | bytes 196640 | tf_op jit(solution)/shard_map/ppermute | solution.py:26
  71.8 4.1 %collective-permute-done.6 = bf16[4,1,64,384]{3,2,1,0:T(8,128)(2,1)S(1)} collective-permute-done((bf16[4,1,64,384]{3,2,1,0:T(8,128)(2,1)S(1)}, bf16[4,1,64,384]{3,2,1,0:T(8,128)(2,1)S(1)}, u32[]{:S(2)}, u32[]{:S(2)}) %collective-permute-start.6) | collective-permute-done | bytes 196640 | tf_op jit(solution)/shard_map/ppermute | solution.py:29
  77.2 1.4 %copy-done.2 = bf16[9,1152,192]{1,2,0:T(8,128)(2,1)S(1)} copy-done((bf16[9,1152,192]{1,2,0:T(8,128)(2,1)S(1)}, bf16[9,1152,192]{1,2,0:T(8,128)(2,1)}, u32[]{:S(2)}) %copy-start.2) | copy-done | bytes 3981336
  83.0 2.1 %all_gather.15 = bf16[2,2,64,384]{2,1,0,3:T(2,128)(2,1)S(1)} all-gather(bf16[2,2,64,192]{2,1,0,3:T(2,128)(2,1)S(1)} %copy.37), channel_id=1, replica_groups=mesh['groups'=2,'space'=4,'tm'=2,'chan'=2] {'chan'}, dimensions={3}, use_global_device_ids=true | all-gather | bytes 294912 | tf_op jit(solution)/shard_map/all_gather | solution.py:75
  85.6 3.6 %collective-permute-start.7 = (bf16[2,1,64,384]{2,1,0,3:T(2,128)(2,1)S(1)}, bf16[2,1,64,384]{2,1,0,3:T(2,128)(2,1)S(1)}, u32[]{:S(2)}, u32[]{:S(2)}) collective-permute-start(bf16[2,1,64,384]{2,1,0,3:T(2,128)(2,1)S(1)} %get-tuple-element.62), channel_id=1, source_target_pairs={{0,4},{4,8},{8,12},{1,5},{5,9},{9,13},{2,6},{6,10},{10,14},{3,7},{... | collective-permute-start | bytes 294920 | tf_op jit(solution)/shard_map/ppermute | solution.py:26
  89.2 1.5 %collective-permute-start.8 = (bf16[2,1,64,384]{2,1,0,3:T(2,128)(2,1)S(1)}, bf16[2,1,64,384]{2,1,0,3:T(2,128)(2,1)S(1)}, u32[]{:S(2)}, u32[]{:S(2)}) collective-permute-start(bf16[2,1,64,384]{2,1,0,3:T(2,128)(2,1)S(1)} %get-tuple-element.63), channel_id=1, source_target_pairs={{4,0},{8,4},{12,8},{5,1},{9,5},{13,9},{6,2},{10,6},{14,10},{7,3},{... | collective-permute-start | bytes 294920 | tf_op jit(solution)/shard_map/ppermute | solution.py:29
  90.7 7.2 %collective-permute-done.7 = bf16[2,1,64,384]{2,1,0,3:T(2,128)(2,1)S(1)} collective-permute-done((bf16[2,1,64,384]{2,1,0,3:T(2,128)(2,1)S(1)}, bf16[2,1,64,384]{2,1,0,3:T(2,128)(2,1)S(1)}, u32[]{:S(2)}, u32[]{:S(2)}) %collective-permute-start.7) | collective-permute-done | bytes 98336 | tf_op jit(solution)/shard_map/ppermute | solution.py:26
  97.9 4.1 %collective-permute-done.8 = bf16[2,1,64,384]{2,1,0,3:T(2,128)(2,1)S(1)} collective-permute-done((bf16[2,1,64,384]{2,1,0,3:T(2,128)(2,1)S(1)}, bf16[2,1,64,384]{2,1,0,3:T(2,128)(2,1)S(1)}, u32[]{:S(2)}, u32[]{:S(2)}) %collective-permute-start.8) | collective-permute-done | bytes 98336 | tf_op jit(solution)/shard_map/ppermute | solution.py:29
  102.0 1.6 %pad_maximum_fusion.3 = bf16[2,4,64,384]{2,1,0,3:T(4,128)(2,1)S(1)} fusion(bf16[2,1,64,384]{2,1,0,3:T(2,128)(2,1)S(1)} %collective-permute-done.8, bf16[2,2,64,384]{2,1,0,3:T(2,128)(2,1)S(1)} %all_gather.15, bf16[2,1,64,384]{2,1,0,3:T(2,128)(2,1)S(1)} %collective-permute-done.7), kind=kLoop, calls=%fused_computation.45 | loop fusion | flops 1179648 | bytes 786432 | tf_op jit(solution)/shard_map/concatenate | solution.py:30
  105.9 2.6 %pad_slice_fusion.1 = (bf16[2,4,128,384]{3,2,1,0:T(8,128)(2,1)S(1)}, bf16[2,4,128,384]{3,2,1,0:T(8,128)(2,1)S(1)}, bf16[2,4,128,384]{3,2,1,0:T(8,128)(2,1)S(1)},...) fusion(bf16[2,6,128,384]{3,2,1,0:T(8,128)(2,1)S(1)} %reshape.183), kind=kLoop, calls=%fused_computation.47 | loop fusion | bytes 10616832 | tf_op jit(solution)/shard_map/slice | solution.py:38
  (101 shorter events, 26.4 us)
Async XLA Ops:
  0.0 22.1 %copy-start = (bf16[432,192]{0,1:T(8,128)(2,1)S(1)}, bf16[432,192]{0,1:T(8,128)(2,1)}, u32[]{:S(2)}) copy-start(bf16[432,192]{0,1:T(8,128)(2,1)} %param.12) | copy-start | bytes 497668
  15.7 4.8 %collective-permute-start = (bf16[2,4,1024]{2,1,0:T(4,128)(2,1)S(1)}, bf16[2,4,1024]{2,1,0:T(4,128)(2,1)S(1)}, u32[]{:S(2)}, u32[]{:S(2)}) collective-permute-start(bf16[2,4,1024]{2,1,0:T(4,128)(2,1)S(1)} %pad_dynamic-slice_fusion), channel_id=1, source_target_pairs={{0,2},{1,3},{4,6},{5,7},{8,10},{9,11},{12,14},{13,15},{16,18},{17,... | collective-permute-start | bytes 49160 | tf_op jit(solution)/shard_map/ppermute | solution.py:18
  21.1 1.0 copy-start.7
  22.1 3.4 %copy-start.4 = (f32[384]{0:T(512)S(1)}, f32[384]{0:T(512)}, u32[]{:S(2)}) copy-start(f32[384]{0:T(512)} %param.14) | copy-start | bytes 4612
  25.7 8.7 %collective-permute-start.1 = (bf16[2,2,64,384]{3,2,1,0:T(8,128)(2,1)S(1)}, bf16[2,2,64,384]{3,2,1,0:T(8,128)(2,1)S(1)}, u32[]{:S(2)}, u32[]{:S(2)}) collective-permute-start(bf16[2,2,64,384]{3,2,1,0:T(8,128)(2,1)S(1)} %fusion.68), channel_id=1, source_target_pairs={{0,2},{1,3},{4,6},{5,7},{8,10},{9,11},{12,14},{13,15},{16,18},{17,... | collective-permute-start | bytes 589832 | tf_op jit(solution)/shard_map/ppermute | solution.py:18
  34.4 7.1 %collective-permute-start.2 = (bf16[4,1,64,384]{3,2,1,0:T(8,128)(2,1)S(1)}, bf16[4,1,64,384]{3,2,1,0:T(8,128)(2,1)S(1)}, u32[]{:S(2)}, u32[]{:S(2)}) collective-permute-start(bf16[4,1,64,384]{3,2,1,0:T(8,128)(2,1)S(1)} %get-tuple-element.70), channel_id=1, source_target_pairs={{0,4},{4,8},{8,12},{1,5},{5,9},{9,13},{2,6},{6,10},{10,14},{3,7},{... | collective-permute-start | bytes 589832 | tf_op jit(solution)/shard_map/ppermute | solution.py:26
  38.0 7.7 %collective-permute-start.3 = (bf16[4,1,64,384]{3,2,1,0:T(8,128)(2,1)S(1)}, bf16[4,1,64,384]{3,2,1,0:T(8,128)(2,1)S(1)}, u32[]{:S(2)}, u32[]{:S(2)}) collective-permute-start(bf16[4,1,64,384]{3,2,1,0:T(8,128)(2,1)S(1)} %get-tuple-element.71), channel_id=1, source_target_pairs={{4,0},{8,4},{12,8},{5,1},{9,5},{13,9},{6,2},{10,6},{14,10},{7,3},{... | collective-permute-start | bytes 589832 | tf_op jit(solution)/shard_map/ppermute | solution.py:29
  46.6 2.1 %copy-start.1 = (bf16[9,1152,192]{1,2,0:T(8,128)(2,1)S(1)}, bf16[9,1152,192]{1,2,0:T(8,128)(2,1)}, u32[]{:S(2)}) copy-start(bf16[9,1152,192]{1,2,0:T(8,128)(2,1)} %param.15) | copy-start | bytes 11943940
  51.8 0.7 copy-start.8
  52.5 3.5 %copy-start.5 = (f32[384]{0:T(512)S(1)}, f32[384]{0:T(512)}, u32[]{:S(2)}) copy-start(f32[384]{0:T(512)} %param.17) | copy-start | bytes 4612
  56.2 8.8 %collective-permute-start.4 = (bf16[2,2,64,384]{3,2,1,0:T(8,128)(2,1)S(1)}, bf16[2,2,64,384]{3,2,1,0:T(8,128)(2,1)S(1)}, u32[]{:S(2)}, u32[]{:S(2)}) collective-permute-start(bf16[2,2,64,384]{3,2,1,0:T(8,128)(2,1)S(1)} %fusion.76), channel_id=1, source_target_pairs={{0,2},{1,3},{4,6},{5,7},{8,10},{9,11},{12,14},{13,15},{16,18},{17,... | collective-permute-start | bytes 589832 | tf_op jit(solution)/shard_map/ppermute | solution.py:18
  65.1 6.7 %collective-permute-start.5 = (bf16[4,1,64,384]{3,2,1,0:T(8,128)(2,1)S(1)}, bf16[4,1,64,384]{3,2,1,0:T(8,128)(2,1)S(1)}, u32[]{:S(2)}, u32[]{:S(2)}) collective-permute-start(bf16[4,1,64,384]{3,2,1,0:T(8,128)(2,1)S(1)} %get-tuple-element.66), channel_id=1, source_target_pairs={{0,4},{4,8},{8,12},{1,5},{5,9},{9,13},{2,6},{6,10},{10,14},{3,7},{... | collective-permute-start | bytes 589832 | tf_op jit(solution)/shard_map/ppermute | solution.py:26
  68.2 7.7 %collective-permute-start.6 = (bf16[4,1,64,384]{3,2,1,0:T(8,128)(2,1)S(1)}, bf16[4,1,64,384]{3,2,1,0:T(8,128)(2,1)S(1)}, u32[]{:S(2)}, u32[]{:S(2)}) collective-permute-start(bf16[4,1,64,384]{3,2,1,0:T(8,128)(2,1)S(1)} %get-tuple-element.67), channel_id=1, source_target_pairs={{4,0},{8,4},{12,8},{5,1},{9,5},{13,9},{6,2},{10,6},{14,10},{7,3},{... | collective-permute-start | bytes 589832 | tf_op jit(solution)/shard_map/ppermute | solution.py:29
  76.5 2.1 %copy-start.2 = (bf16[9,1152,192]{1,2,0:T(8,128)(2,1)S(1)}, bf16[9,1152,192]{1,2,0:T(8,128)(2,1)}, u32[]{:S(2)}) copy-start(bf16[9,1152,192]{1,2,0:T(8,128)(2,1)} %param.18) | copy-start | bytes 11943940
  81.6 0.7 copy-start.9
  85.6 12.3 %collective-permute-start.7 = (bf16[2,1,64,384]{2,1,0,3:T(2,128)(2,1)S(1)}, bf16[2,1,64,384]{2,1,0,3:T(2,128)(2,1)S(1)}, u32[]{:S(2)}, u32[]{:S(2)}) collective-permute-start(bf16[2,1,64,384]{2,1,0,3:T(2,128)(2,1)S(1)} %get-tuple-element.62), channel_id=1, source_target_pairs={{0,4},{4,8},{8,12},{1,5},{5,9},{9,13},{2,6},{6,10},{10,14},{3,7},{... | collective-permute-start | bytes 294920 | tf_op jit(solution)/shard_map/ppermute | solution.py:26
  89.2 12.8 %collective-permute-start.8 = (bf16[2,1,64,384]{2,1,0,3:T(2,128)(2,1)S(1)}, bf16[2,1,64,384]{2,1,0,3:T(2,128)(2,1)S(1)}, u32[]{:S(2)}, u32[]{:S(2)}) collective-permute-start(bf16[2,1,64,384]{2,1,0,3:T(2,128)(2,1)S(1)} %get-tuple-element.63), channel_id=1, source_target_pairs={{4,0},{8,4},{12,8},{5,1},{9,5},{13,9},{6,2},{10,6},{14,10},{7,3},{... | collective-permute-start | bytes 294920 | tf_op jit(solution)/shard_map/ppermute | solution.py:29
  108.6 1.1 copy-start.3
  111.7 0.7 copy-start.6
where the time goes:
time: 114 us
  waiting for transfers between devices  34.4 us (30%)
  starting transfers between devices  26.4 us (23%)
  blocking collectives  21.2 us (19%)
  local copies, waits for them, and re-layouts  16.9 us (15%)
  matrix products  9.15 us (8%)
  other arithmetic  5.26 us (5%)
    all_gather x1, blocking collectives, shards(): gathered = lax.all_gather(latent, 'space', axis=1, tiled=True)  14.9 us
    ppermute x3, waiting for transfers between devices, padded_2(): lax.ppermute(lax.slice_in_dim(block, 0, width, axis=dim), axis, backward)  12.4 us
    ppermute x3, starting transfers between devices, passed_along(): return lax.ppermute(array, axis, pairs)  12 us
    ppermute x3, waiting for transfers between devices, padded_2(): lax.ppermute(lax.slice_in_dim(block, block.shape[dim] - width, None, axis...  11.7 us
    ppermute x3, starting transfers between devices, padded_2(): lax.ppermute(lax.slice_in_dim(block, block.shape[dim] - width, None, axis...  10.3 us
    ppermute x3, waiting for transfers between devices, passed_along(): return lax.ppermute(array, axis, pairs)  10.3 us
    dot_general x21, matrix products, conv_taps(): jnp.dot(tap_cols, weight[tap_index].reshape(-1, out_chan), preferred_elem...  8.9 us
    all_gather x3, blocking collectives, join_chan(): return lax.all_gather(own_part, 'chan', axis=3, tiled=True)  6.26 us
  transfers between devices with their start and end apart: 9, of which 9 were waited for; matrix products, arithmetic and copies ran while one was open for 0% of the time, Pallas kernels for 0%

commit v1 on v0

v1 whole, which is shorter than its diff:
```python
import functools

import jax
import jax.numpy as jnp
from jax import lax
from jax.experimental import pallas as pl
from jax.experimental.pallas import tpu as pltpu
from jax.sharding import PartitionSpec as P

ZC = 16
C = 384
FS = 2
LW = 64
LANES = 128
WIDE = 256

epsilon = 1e-06


def activated(values, gain_half):
    squares = jnp.sum(values * values, axis=-1, keepdims=True)
    half = values * lax.rsqrt(squares * (1.0 / C) + epsilon) * gain_half
    return half + half * jnp.tanh(half)


def store_width_taps(target, frame, act, rows):
    act = act.reshape(rows, LW, C)
    column = lax.broadcasted_iota(jnp.int32, act.shape, 1)
    left = jnp.where(column == 0, 0.0, pltpu.roll(act, 1, 1))
    right = jnp.where(column == LW - 1, 0.0, pltpu.roll(act, LW - 1, 1))
    target[frame, :, :, 0:C] = left.astype(jnp.bfloat16)
    target[frame, :, :, C : 2 * C] = act.astype(jnp.bfloat16)
    target[frame, :, :, 2 * C :] = right.astype(jnp.bfloat16)


def masked_rows(act, rows, first_row, frame_ok, height):
    act = act.reshape(rows, LW, C)
    row = lax.broadcasted_iota(jnp.int32, act.shape, 0) + first_row
    keep = (row >= 0) & (row < height) & frame_ok
    return jnp.where(keep, act, 0.0).reshape(rows * LW, C)


def joined(low, high):
    lane = lax.broadcasted_iota(jnp.int32, (low.shape[0], LANES), 1)
    middle = jnp.where(lane < LANES // 2, low[:, LANES:], high[:, :LANES])
    return jnp.concatenate([low[:, :LANES], middle, high[:, LANES:]], axis=-1)


def packed(half, chan):
    return jnp.where(chan == 0, half, pltpu.roll(half, WIDE - C // 2, 1))


def halves(own, other, chan):
    own = own.astype(jnp.float32)
    other = other.astype(jnp.float32)
    return joined(jnp.where(chan == 0, own, other), jnp.where(chan == 0, other, own))


def conv_into(acc, taps, weight, starts, out_frames, out_rows):
    width = weight.shape[1]
    block = out_rows * LW
    acc[:, 0:width] = jnp.zeros((acc.shape[0], width), jnp.float32)
    for depth_at in (2, 1, 0):
        skip = max(0, -(starts + depth_at))
        count = out_frames - skip
        if count <= 0:
            continue
        first = starts + depth_at + skip
        for row_at in range(3):
            lhs = taps[first : first + count, row_at : row_at + out_rows]
            product = lax.dot_general(
                lhs.reshape(count * block, 3 * C),
                weight[depth_at * 3 + row_at],
                (((1,), (1,)), ((), ())),
                preferred_element_type=jnp.float32,
            )
            acc[skip * block :, 0:width] += product


def first_stage(
    dims, lat, win, bias, gain, weight, conv_bias, second, residual, window, taps, acc
):
    tm_count, rows_here, height, early = dims
    early_in, early_one, early_two = early
    space = lax.axis_index("space")
    section = lax.axis_index("tm")
    chan = lax.axis_index("chan")
    row0 = space * rows_here
    groups = LW * ZC // LANES
    lane = lax.broadcasted_iota(jnp.int32, (groups, LANES), 1)
    group = lax.broadcasted_iota(jnp.int32, (groups, LANES), 0)
    low = lane < LANES // 2
    frames_in = FS + early_in
    rows_in = rows_here + 8

    for frame in range(frames_in):
        frame_abs = section * FS - early_in + frame
        for row in range(rows_in):
            row_abs = row0 - 4 + row
            ok = (frame_abs >= 0) & (row_abs >= 0) & (row_abs < height)
            at = jnp.where(ok, frame_abs * height + row_abs, 0)
            here = jnp.where(ok, lat[at], 0.0)
            before = jnp.where(group == 0, 0.0, pltpu.roll(here, 1, 0))
            after = jnp.where(group == groups - 1, 0.0, pltpu.roll(here, groups - 1, 0))
            for col in range(8):
                source = here
                if col == 0:
                    source = jnp.where(lane >= LANES - ZC, before, here)
                if col == 7:
                    source = jnp.where(lane < ZC, after, here)
                shift = (-ZC * (col - 1)) % LANES
                one = source if shift == 0 else pltpu.roll(source, shift, 1)
                two = pltpu.roll(source, (shift + LANES // 2) % LANES, 1)
                window.at[frame, row][pl.ds(col, groups, stride=8), :] = jnp.where(low, one, two)

    rows_one = rows_here + 6
    voxels = rows_one * LW
    lane_wide = lax.broadcasted_iota(jnp.int32, (rows_one, LW, LANES), 2)
    half_gain = gain[...] * 0.5
    for frame in range(FS + early_one):
        slots = []
        for depth_at in (2, 1, 0):
            source = frame - early_one - 2 + depth_at + early_in
            if source >= 0:
                slots += [(source, row_at) for row_at in range(3)]
        pieces = []
        for pair in range(0, len(slots), 2):
            source, row_at = slots[pair]
            value = window[source, row_at : row_at + rows_one]
            second_slot = 0.0
            if pair + 1 < len(slots):
                source, row_at = slots[pair + 1]
                second_slot = window[source, row_at : row_at + rows_one]
            value = jnp.where(lane_wide < LANES // 2, value, second_slot)
            pieces.append(value.astype(jnp.bfloat16).reshape(voxels, LANES))
        lhs = jnp.concatenate(pieces, axis=-1)
        out = jnp.dot(lhs, win[0 : lhs.shape[1]], preferred_element_type=jnp.float32)
        out = (out + bias[...]).astype(jnp.bfloat16)
        if frame >= early_one:
            inner = out[2 * LW : (rows_one - 2) * LW].astype(jnp.float32)
            mine = jnp.where(
                chan == 0, inner[:, :WIDE], pltpu.roll(inner[:, LANES:], C // 2, 1)
            )
            residual[frame - early_one] = mine.astype(jnp.bfloat16)
        act = activated(out.astype(jnp.float32), half_gain)
        frame_ok = section * FS - early_one + frame >= 0
        act = masked_rows(act, rows_one, row0 - 3, frame_ok, height)
        store_width_taps(taps, frame, act, rows_one)

    conv_into(
        acc, taps, weight, early_one - early_two - 2, FS + early_two, rows_here + 4
    )
    second[...] = packed(acc[...] + conv_bias[...], chan).astype(jnp.bfloat16)


def second_stage(
    dims, own, other, residual, gain, weight, conv_bias, block, taps, acc
):
    tm_count, rows_here, height, early_two = dims
    section = lax.axis_index("tm")
    chan = lax.axis_index("chan")
    row0 = lax.axis_index("space") * rows_here
    rows_two = rows_here + 4
    voxels = rows_two * LW
    half_gain = gain[...] * 0.5
    for frame in range(FS + early_two):
        span = pl.ds(frame * voxels, voxels)
        values = halves(own[span, :], other[span, :], chan)
        act = activated(values, half_gain)
        frame_ok = section * FS - early_two + frame >= 0
        act = masked_rows(act, rows_two, row0 - 2, frame_ok, height)
        store_width_taps(taps, frame, act, rows_two)
    conv_into(acc, taps, weight, early_two - 2, FS, rows_here + 2)
    total = acc[...] + conv_bias[...] + residual[...].astype(jnp.float32)
    block[...] = packed(total, chan).astype(jnp.bfloat16)


def third_stage(dims, own, other, weight, up_bias, decoded, taps):
    rows_here, height = dims
    chan = lax.axis_index("chan")
    row0 = lax.axis_index("space") * rows_here
    rows_three = rows_here + 2
    voxels = rows_three * LW
    out_chan = weight.shape[2] // 2
    for frame in range(FS):
        span = pl.ds(frame * voxels, voxels)
        values = halves(own[span, :], other[span, :], chan)
        values = masked_rows(values, rows_three, row0 - 1, True, height)
        store_width_taps(taps, frame, values, rows_three)
    count = FS * rows_here * LW
    source = lax.broadcasted_iota(jnp.int32, (4 * LW, 4 * LW), 0)
    target = lax.broadcasted_iota(jnp.int32, (4 * LW, 4 * LW), 1)
    phase = source // (2 * LW)
    place = source % (2 * LW)
    wanted = (place // LW) * (2 * LW) + (place % LW) * 2 + phase
    shuffle = jnp.where(wanted == target, 1.0, 0.0).astype(jnp.bfloat16)
    for row_phase in range(2):
        total = jnp.zeros((2 * out_chan, count), jnp.float32)
        for row_at in range(2):
            at = row_phase + row_at
            lhs = taps[:, at : at + rows_here].reshape(count, 3 * C)
            total = total + lax.dot_general(
                weight[row_phase, row_at],
                lhs,
                (((1,), (1,)), ((), ())),
                preferred_element_type=jnp.float32,
            )
        for frame in range(FS):
            for row in range(0, rows_here, 2):
                start = (frame * rows_here + row) * LW
                part = total[:, start : start + 2 * LW]
                pair = jnp.concatenate([part[:out_chan], part[out_chan:]], axis=-1)
                pair = (pair + up_bias[...]).astype(jnp.bfloat16)
                pixels = jnp.dot(pair, shuffle, preferred_element_type=jnp.float32)
                pixels = pixels.astype(jnp.bfloat16)
                decoded[frame, 2 * row + row_phase] = pixels[:, : 2 * LW]
                decoded[frame, 2 * row + 2 + row_phase] = pixels[:, 2 * LW :]


def in_vmem(count):
    return [pl.BlockSpec(memory_space=pltpu.VMEM)] * count


def up_phases(up_weight):
    w = jnp.swapaxes(up_weight, 1, 2).astype(jnp.float32)
    w = [[w[b, :, c * C : (c + 1) * C] for c in range(3)] for b in range(3)]
    out = []
    for top, bottom in (((0,), (1, 2)), ((0, 1), (2,))):
        for rows in (top, bottom):
            cols = [sum(w[b][c] for b in rows) for c in range(3)]
            zero = jnp.zeros_like(cols[0])
            even = jnp.concatenate([cols[0], cols[1] + cols[2], zero], axis=1)
            odd = jnp.concatenate([zero, cols[0] + cols[1], cols[2]], axis=1)
            out.append(jnp.concatenate([even, odd], axis=0))
    return jnp.stack(out).reshape(2, 2, -1, 3 * C).astype(jnp.bfloat16)


def shards(
    latent,
    in_weight,
    in_bias,
    first_gain,
    first_weight,
    first_bias,
    second_gain,
    second_weight,
    second_bias,
    up_weight,
    up_bias,
):
    space_count = lax.axis_size("space")
    tm_count = lax.axis_size("tm")
    chan = lax.axis_index("chan")
    rows_here = latent.shape[1] // FS
    height = rows_here * space_count
    groups = LW * ZC // LANES
    half = C // 2
    earlier = FS * (tm_count - 1)
    early_two, early_one, early_in = min(2, earlier), min(4, earlier), min(6, earlier)
    swap = [(0, 1), (1, 0)]

    piece = latent.reshape(1, FS * rows_here * groups, LANES).astype(jnp.float32)
    piece = jnp.broadcast_to(piece, (tm_count * space_count,) + piece.shape[1:])
    lat = lax.all_to_all(piece, ("tm", "space"), 0, 0, tiled=True)
    lat = lat.reshape(tm_count * FS * height, groups, LANES)

    other_weight = lax.ppermute(in_weight, "chan", swap)
    other_bias = lax.ppermute(in_bias, "chan", swap)
    win = jnp.where(
        chan == 0,
        jnp.concatenate([in_weight, other_weight], axis=1),
        jnp.concatenate([other_weight, in_weight], axis=1),
    )
    win = win.reshape(3, 3, 3 * ZC, C)[::-1].reshape(9, 3 * ZC, C)
    win = jnp.pad(win, ((0, 1), (0, LANES // 2 - 3 * ZC), (0, 0))).reshape(5 * LANES, C)
    bias = jnp.where(
        chan == 0,
        jnp.concatenate([in_bias, other_bias]),
        jnp.concatenate([other_bias, in_bias]),
    ).reshape(1, C)

    def wide(vector):
        return jnp.pad(vector, (0, WIDE - half)).reshape(1, WIDE)

    voxels_two = (FS + early_two) * (rows_here + 4) * LW
    voxels_three = FS * (rows_here + 2) * LW
    second_own, residual = pl.pallas_call(
        functools.partial(
            first_stage, (tm_count, rows_here, height, (early_in, early_one, early_two))
        ),
        out_shape=(
            jax.ShapeDtypeStruct((voxels_two, WIDE), jnp.bfloat16),
            jax.ShapeDtypeStruct((FS, (rows_here + 2) * LW, WIDE), jnp.bfloat16),
        ),
        in_specs=in_vmem(6),
        out_specs=tuple(in_vmem(2)),
        scratch_shapes=[
            pltpu.VMEM((FS + early_in, rows_here + 8, LW, LANES), jnp.float32),
            pltpu.VMEM((FS + early_one, rows_here + 6, LW, 3 * C), jnp.bfloat16),
            pltpu.VMEM((voxels_two, WIDE), jnp.float32),
        ],
        name="first_stage",
    )(lat, win, bias, first_gain.reshape(1, C), jnp.swapaxes(first_weight, 1, 2), wide(first_bias))
    second_other = lax.ppermute(second_own, "chan", swap)

    block_own = pl.pallas_call(
        functools.partial(second_stage, (tm_count, rows_here, height, early_two)),
        out_shape=jax.ShapeDtypeStruct((voxels_three, WIDE), jnp.bfloat16),
        in_specs=in_vmem(6),
        out_specs=in_vmem(1)[0],
        scratch_shapes=[
            pltpu.VMEM((FS + early_two, rows_here + 4, LW, 3 * C), jnp.bfloat16),
            pltpu.VMEM((voxels_three, WIDE), jnp.float32),
        ],
        name="second_stage",
    )(
        second_own,
        second_other,
        residual.reshape(voxels_three, WIDE),
        second_gain.reshape(1, C),
        jnp.swapaxes(second_weight, 1, 2),
        wide(second_bias),
    )
    block_other = lax.ppermute(block_own, "chan", swap)

    out_chan = up_weight.shape[-1]
    return pl.pallas_call(
        functools.partial(third_stage, (rows_here, height)),
        out_shape=jax.ShapeDtypeStruct((FS, 2 * rows_here, out_chan, 2 * LW), jnp.bfloat16),
        in_specs=in_vmem(4),
        out_specs=in_vmem(1)[0],
        scratch_shapes=[pltpu.VMEM((FS, rows_here + 2, LW, 3 * C), jnp.bfloat16)],
        name="third_stage",
    )(block_own, block_other, up_phases(up_weight), up_bias.reshape(out_chan, 1))


def solution(mesh):
    placed = (
        P(("groups", "tm"), "space", None),
        P(None, "chan"),
        P("chan"),
        P(),
        P(None, None, "chan"),
        P("chan"),
        P(),
        P(None, None, "chan"),
        P("chan"),
        P(None, None, "chan"),
        P("chan"),
    )
    return jax.shard_map(
        shards,
        mesh=mesh,
        in_specs=placed,
        out_specs=P(("groups", "tm"), "space", "chan", None),
        check_vma=False,
    )
```

time: 114 us -> 50 us (0.44)
  waiting for transfers between devices: 34.4 us -> 3.68 us
  Pallas kernels: 0 us -> 25.2 us
  blocking collectives: 21.2 us -> 0 us
  starting transfers between devices: 26.4 us -> 8.08 us
  matrix products: 9.15 us -> 0 us
  local copies, waits for them, and re-layouts: 16.9 us -> 8.66 us
  other arithmetic: 5.26 us -> 3.95 us
    ppermute x9 -> x4, waiting for transfers between devices: 34.4 us -> 0.31 us  [the longest x1 0.3 us: shards(): second_other = lax.ppermute(second_own, 'chan', swap)]
    ppermute x9 -> x4, starting transfers between devices: 26.4 us -> 0.86 us  [the longest x1 0.56 us: shards(): other_weight = lax.ppermute(in_weight, 'chan', swap)]
    pallas_call x0 -> x3, Pallas kernels: none -> 25.2 us  [the longest x1 13.3 us: shards(): pl.pallas_call(functools.partial(first_stage, (tm_count, rows_here, heigh...]
    all_gather x4 -> x0, blocking collectives: 21.2 us -> none  [the longest x1 14.9 us: shards(): gathered = lax.all_gather(latent, 'space', axis=1, tiled=True)]
    dot_general x22 -> x0, matrix products: 9.15 us -> none  [the longest x21 8.9 us: conv_taps(): jnp.dot(tap_cols, weight[tap_index].reshape(-1, out_chan), preferred_elem...]
    all_to_all x0 -> x1, starting transfers between devices: none -> 7.22 us  [shards(): lat = lax.all_to_all(piece, ('tm', 'space'), 0, 0, tiled=True)]
    slice x11 -> x0, local copies, waits for them, and re-layouts: 5.2 us -> none  [the longest x3 3.92 us: width_taps(): tap_slab[..., 0:col_count, :]]
    concatenate x25 -> x0, other arithmetic: 4.64 us -> none  [the longest x5 2.49 us: padded_2(): block = jnp.concatenate([low, block, high], axis=dim)]
  transfers between devices with their start and end apart: 9 -> 5, of which waited for: 9 -> 2; matrix products, arithmetic and copies ran while one was open for 0% -> 19% of each run, Pallas kernels for 0% -> 0%
where the time goes in v1:
time: 50 us; the launch traced here: 49.6 us
  Pallas kernels  25.2 us (50%)
  local copies, waits for them, and re-layouts  8.66 us (17%)
  starting transfers between devices  8.08 us (16%)
  other arithmetic  3.95 us (8%)
  waiting for transfers between devices  3.68 us (7%)
    pallas_call x1, Pallas kernels, shards(): pl.pallas_call(functools.partial(first_stage, (tm_count, rows_here, heigh...  13.3 us
    pallas_call x1, Pallas kernels, shards(): pl.pallas_call(functools.partial(second_stage, (tm_count, rows_here, heig...  7.67 us
    all_to_all x1, starting transfers between devices, shards(): lat = lax.all_to_all(piece, ('tm', 'space'), 0, 0, tiled=True)  7.22 us
    pallas_call x1, Pallas kernels, shards(): pl.pallas_call(functools.partial(third_stage, (rows_here, height)), out_s...  4.21 us
    all_to_all x1, waiting for transfers between devices, shards(): lat = lax.all_to_all(piece, ('tm', 'space'), 0, 0, tiled=True)  3.37 us
    unnamed x19, local copies, waits for them, and re-layouts  3.34 us
    another operation x3, other arithmetic, up_phases(): return jnp.stack(out).reshape(2, 2, -1, 3 * C).astype(jnp.bfloat16)  1.68 us
    convert_element_type x1, other arithmetic, up_phases(): w = jnp.swapaxes(up_weight, 1, 2).astype(jnp.float32)  1.19 us
  transfers between devices with their start and end apart: 5, of which 2 were waited for; matrix products, arithmetic and copies ran while one was open for 19% of the time, Pallas kernels for 0%

profile of v1, /device:TPU:0, one launch (start us, length us, event | category | flops | bytes accessed | tf_op | source)
XLA Modules:
  0.0 49.6 jit_solution(12018441830064278579)
XLA Ops:
  0.0 1.1 %copy.14 = bf16[432,192]{1,0:T(8,128)(2,1)S(1)} copy(bf16[432,192]{0,1:T(8,128)(2,1)} %param.12) | data formatting | bytes 331776 | tf_op args[1]
  1.1 0.6 %collective-permute-start = (bf16[432,192]{1,0:T(8,128)(2,1)S(1)}, bf16[432,192]{1,0:T(8,128)(2,1)S(1)}, u32[]{:S(2)}, u32[]{:S(2)}) collective-permute-start(bf16[432,192]{1,0:T(8,128)(2,1)S(1)} %copy.14), channel_id=1, source_target_pairs={{0,1},{1,0},{2,3},{3,2},{4,5},{5,4},{6,7},{7,6},{8,9},{9,8},{10,11... | collective-permute-start | bytes 497672 | tf_op jit(solution)/shard_map/ppermute | solution.py:267
  1.7 0.7 %reshape.109 = f32[32,128]{1,0:T(8,128)S(1)} reshape(bf16[1,4,1024]{2,1,0:T(4,128)(2,1)} %param.11) | data formatting | bytes 24576 | tf_op jit(solution)/shard_map/convert_element_type | solution.py:262
  2.4 0.7 %broadcast_in_dim.2 = f32[8,32,128]{2,1,0:T(8,128)} broadcast(f32[32,128]{1,0:T(8,128)S(1)} %reshape.109), dimensions={1,2} | broadcast | bytes 147456 | tf_op jit(solution)/shard_map/broadcast_in_dim | solution.py:263
  3.1 7.2 %all-to-all-start = ((f32[8,32,128]{2,1,0:T(8,128)}), f32[8,32,128]{2,1,0:T(8,128)S(1)}, u32[]{:S(2)}, u32[]{:S(2)}) async-start(f32[8,32,128]{2,1,0:T(8,128)} %broadcast_in_dim.2), calls=%async_computation | async-start | bytes 262144 | tf_op jit(solution)/shard_map/all_to_all | solution.py:264
  10.3 1.2 %convert_bitcast_fusion = f32[3,96,1152]{2,1,0:T(8,128)S(1)} fusion(bf16[3,1152,96]{1,2,0:T(8,128)(2,1)} %param.20), kind=kLoop, calls=%fused_computation.1 | loop fusion | flops 331776 | bytes 1990656 | tf_op jit(solution)/shard_map/convert_element_type | solution.py:225
  11.6 0.6 %reshape.103.gain = f32[1,384]{1,0:T(1,128)} reshape(f32[384]{0:T(512)S(1)} %copy-done.3) | data formatting | bytes 3072 | tf_op jit(solution)/shard_map/reshape | solution.py:303
  12.2 0.6 %pad.12 = f32[256]{0:T(256)} pad(f32[192]{0:T(256)S(1)} %copy-done.5, f32[]{:T(128)} %constant.11.clone.1), padding=0_64 | pad | bytes 1796 | tf_op jit(solution)/shard_map/jit(_pad)/pad | solution.py:283
  12.8 0.6 %broadcast_select_fusion.bias = f32[1,384]{1,0:T(1,128)} fusion(pred[]{:T(512)S(6)} %eq.4, f32[1,192]{1,0:T(1,128)S(1)} %bitcast.68, f32[1,192]{1,0:T(1,128)S(1)} %bitcast.67), kind=kLoop, calls=%fused_computation.57 | loop fusion | flops 1152 | bytes 3073 | tf_op jit(solution)/shard_map/jit(_where)/select_n | solution.py:276
  13.4 0.3 maximum_select_fusion
  13.7 0.8 %pad.11 = bf16[10,64,384]{2,1,0:T(8,128)(2,1)} pad(bf16[9,48,384]{2,1,0:T(8,128)(2,1)S(1)} %bitcast.60, bf16[]{:T(256)} %constant.10.clone.1), padding=0_1x0_16x0_0 | pad | bytes 823298 | tf_op jit(solution)/shard_map/jit(_pad)/pad | solution.py:275
  14.6 3.4 %all-to-all-done = f32[8,32,128]{2,1,0:T(8,128)S(1)} async-done(((f32[8,32,128]{2,1,0:T(8,128)}), f32[8,32,128]{2,1,0:T(8,128)S(1)}, u32[]{:S(2)}, u32[]{:S(2)}) %all-to-all-start) | async-done | bytes 131104 | tf_op jit(solution)/shard_map/all_to_all | solution.py:264
  18.0 0.7 %copy-done.1 = f32[8,32,128]{2,1,0:T(8,128)} copy-done((f32[8,32,128]{2,1,0:T(8,128)}, f32[8,32,128]{2,1,0:T(8,128)S(1)}, u32[]{:S(2)}) %copy-start.1) | copy-done | bytes 131096
  18.6 13.3 %first_stage.1 = (bf16[1536,256]{1,0:T(8,128)(2,1)}, bf16[2,256,256]{2,1,0:T(8,128)(2,1)}) custom-call(f32[32,8,128]{2,1,0:T(8,128)} %bitcast.62, bf16[640,384]{1,0:T(8,128)(2,1)} %bitcast.59, f32[1,384]{1,0:T(1,128)} %broadcast_select_fusion.bias, f32[1,384]{1,0:T(1,128)} %reshape.103.gain, bf16[9,192,1152]{2,1,0:T(8,128)(2,1)} %bitcast.58, f32[1,256]{1,0:T(1,128)} %bitcast.66), custom_call_target="tpu_custom_call" | custom-call | tf_op jit(solution)/shard_map/first_stage/pallas_call | solution.py:287
  32.0 0.6 %reshape.106.gain = f32[1,384]{1,0:T(1,128)} reshape(f32[384]{0:T(512)S(1)} %copy-done.4) | data formatting | bytes 3072 | tf_op jit(solution)/shard_map/reshape | solution.py:320
  32.5 0.6 %pad.13 = f32[256]{0:T(256)} pad(f32[192]{0:T(256)S(1)} %copy-done.6, f32[]{:T(128)} %constant.11.clone.1), padding=0_64 | pad | bytes 1796 | tf_op jit(solution)/shard_map/jit(_pad)/pad | solution.py:283
  33.1 0.7 %copy.16.up_bias = f32[96,1]{1,0:T(8,128)} copy(f32[96,1]{0,1:T(1,128)S(1)} %bitcast.69) | data formatting | bytes 768 | tf_op jit(solution)/shard_map/reshape | solution.py:334
  34.1 0.3 collective-permute-done.2.other
  34.4 0.9 %copy-done = bf16[1536,256]{1,0:T(8,128)(2,1)} copy-done((bf16[1536,256]{1,0:T(8,128)(2,1)}, bf16[1536,256]{1,0:T(8,128)(2,1)S(1)}, u32[]{:S(2)}) %copy-start) | copy-done | bytes 786456
  35.3 7.7 %second_stage.1.own = bf16[512,256]{1,0:T(8,128)(2,1)} custom-call(bf16[1536,256]{1,0:T(8,128)(2,1)} %get-tuple-element.7.own, bf16[1536,256]{1,0:T(8,128)(2,1)} %copy-done, bf16[512,256]{1,0:T(8,128)(2,1)} %bitcast.63, f32[1,384]{1,0:T(1,128)} %reshape.106.gain, bf16[9,192,1152]{2,1,0:T(8,128)(2,1)} %bitcast.57, f32[1,256]{1,0:T(1,128)} %bitcast.65), custom_call_target="tpu_custom_call" | custom-call | tf_op jit(solution)/shard_map/second_stage/pallas_call | solution.py:306
  43.0 0.2 collective-permute-start.3
  43.2 1.5 %pad_maximum_fusion = bf16[4,192,1152]{2,1,0:T(8,128)(2,1)} fusion(bf16[1,192,1152]{2,1,0:T(8,128)(2,1)S(1)} %get-tuple-element.26, bf16[1,192,1152]{2,1,0:T(8,128)(2,1)S(1)} %get-tuple-element.27, bf16[1,192,1152]{2,1,0:T(8,128)(2,1)S(1)} %fusion.3, bf16[1,192,1152]{2,1,0:T(8,128)(2,1)S(1)} %get-tuple-element.25), kind=kLoop, calls=%fused_computation | loop fusion | flops 2654208 | bytes 3538944 | tf_op jit(solution)/shard_map/stack | solution.py:235
  44.7 0.7 %copy-done.2 = bf16[512,256]{1,0:T(8,128)(2,1)} copy-done((bf16[512,256]{1,0:T(8,128)(2,1)}, bf16[512,256]{1,0:T(8,128)(2,1)S(1)}, u32[]{:S(2)}) %copy-start.2) | copy-done | bytes 262168
  45.4 4.2 %third_stage.1 = bf16[2,4,96,128]{3,2,1,0:T(8,128)(2,1)} custom-call(bf16[512,256]{1,0:T(8,128)(2,1)} %second_stage.1.own, bf16[512,256]{1,0:T(8,128)(2,1)} %copy-done.2, bf16[2,2,192,1152]{3,2,1,0:T(8,128)(2,1)} %bitcast.56, f32[96,1]{1,0:T(8,128)} %copy.16.up_bias), custom_call_target="tpu_custom_call" | custom-call | tf_op jit(solution)/shard_map/third_stage/pallas_call | solution.py:327
  (27 shorter events, 0.5 us)
Async XLA Ops:
  1.1 12.4 %collective-permute-start = (bf16[432,192]{1,0:T(8,128)(2,1)S(1)}, bf16[432,192]{1,0:T(8,128)(2,1)S(1)}, u32[]{:S(2)}, u32[]{:S(2)}) collective-permute-start(bf16[432,192]{1,0:T(8,128)(2,1)S(1)} %copy.14), channel_id=1, source_target_pairs={{0,1},{1,0},{2,3},{3,2},{4,5},{5,4},{6,7},{7,6},{8,9},{9,8},{10,11... | collective-permute-start | bytes 497672 | tf_op jit(solution)/shard_map/ppermute | solution.py:267
  1.6 11.2 %collective-permute-start.1 = (f32[192]{0:T(256)}, f32[192]{0:T(256)S(1)}, u32[]{:S(2)}, u32[]{:S(2)}) collective-permute-start(f32[192]{0:T(256)} %param.13), channel_id=1, source_target_pairs={{0,1},{1,0},{2,3},{3,2},{4,5},{5,4},{6,7},{7,6},{8,9},{9,8},{10,11... | collective-permute-start | bytes 2312 | tf_op jit(solution)/shard_map/ppermute | solution.py:268
  3.1 14.9 %all-to-all-start = ((f32[8,32,128]{2,1,0:T(8,128)}), f32[8,32,128]{2,1,0:T(8,128)S(1)}, u32[]{:S(2)}, u32[]{:S(2)}) async-start(f32[8,32,128]{2,1,0:T(8,128)} %broadcast_in_dim.2), calls=%async_computation | async-start | bytes 262144 | tf_op jit(solution)/shard_map/all_to_all | solution.py:264
  10.3 1.3 %copy-start.3 = (f32[384]{0:T(512)S(1)}, f32[384]{0:T(512)}, u32[]{:S(2)}) copy-start(f32[384]{0:T(512)} %param.14) | copy-start | bytes 4612
  10.3 1.9 %copy-start.5 = (f32[192]{0:T(256)S(1)}, f32[192]{0:T(256)}, u32[]{:S(2)}) copy-start(f32[192]{0:T(256)} %param.16) | copy-start | bytes 2308
  10.3 2.5 %copy-start.7 = (f32[192]{0:T(256)S(1)}, f32[192]{0:T(256)}, u32[]{:S(2)}) copy-start(f32[192]{0:T(256)} %param.13) | copy-start | bytes 2308
  18.0 0.7 %copy-start.1 = (f32[8,32,128]{2,1,0:T(8,128)}, f32[8,32,128]{2,1,0:T(8,128)S(1)}, u32[]{:S(2)}) copy-start(f32[8,32,128]{2,1,0:T(8,128)S(1)} %all-to-all-done) | copy-start | bytes 393220
  18.6 13.3 %copy-start.4 = (f32[384]{0:T(512)S(1)}, f32[384]{0:T(512)}, u32[]{:S(2)}) copy-start(f32[384]{0:T(512)} %param.17) | copy-start | bytes 4612
  18.6 13.9 %copy-start.6 = (f32[192]{0:T(256)S(1)}, f32[192]{0:T(256)}, u32[]{:S(2)}) copy-start(f32[192]{0:T(256)} %param.19) | copy-start | bytes 2308
  18.6 14.5 %copy-start.8 = (f32[96]{0:T(128)S(1)}, f32[96]{0:T(128)}, u32[]{:S(2)}) copy-start(f32[96]{0:T(128)} %param.21) | copy-start | bytes 1156
  31.9 2.5 %collective-permute-start.2 = (bf16[1536,256]{1,0:T(8,128)(2,1)}, bf16[1536,256]{1,0:T(8,128)(2,1)S(1)}, u32[]{:S(2)}, u32[]{:S(2)}) collective-permute-start(bf16[1536,256]{1,0:T(8,128)(2,1)} %get-tuple-element.7.own), channel_id=1, source_target_pairs={{0,1},{1,0},{2,3},{3,2},{4,5},{5,4},{6,7},{7,6},{8,9},{9,8},{10,11... | collective-permute-start | bytes 2359304 | tf_op jit(solution)/shard_map/ppermute | solution.py:304
  34.4 0.9 %copy-start = (bf16[1536,256]{1,0:T(8,128)(2,1)}, bf16[1536,256]{1,0:T(8,128)(2,1)S(1)}, u32[]{:S(2)}) copy-start(bf16[1536,256]{1,0:T(8,128)(2,1)S(1)} %collective-permute-done.2.other) | copy-start | bytes 2359300
  43.0 1.7 %collective-permute-start.3 = (bf16[512,256]{1,0:T(8,128)(2,1)}, bf16[512,256]{1,0:T(8,128)(2,1)S(1)}, u32[]{:S(2)}, u32[]{:S(2)}) collective-permute-start(bf16[512,256]{1,0:T(8,128)(2,1)} %second_stage.1.own), channel_id=1, source_target_pairs={{0,1},{1,0},{2,3},{3,2},{4,5},{5,4},{6,7},{7,6},{8,9},{9,8},{10,11... | collective-permute-start | bytes 786440 | tf_op jit(solution)/shard_map/ppermute | solution.py:324
  44.7 0.7 %copy-start.2 = (bf16[512,256]{1,0:T(8,128)(2,1)}, bf16[512,256]{1,0:T(8,128)(2,1)S(1)}, u32[]{:S(2)}) copy-start(bf16[512,256]{1,0:T(8,128)(2,1)S(1)} %collective-permute-done.3.other) | copy-start | bytes 786436

commit v2 on v1

v2 whole, which is shorter than its diff:
```python
import functools

import jax
import jax.numpy as jnp
from jax import lax
from jax.experimental import pallas as pl
from jax.experimental.pallas import tpu as pltpu
from jax.sharding import PartitionSpec as P

ZC = 16
C = 384
FS = 2
LW = 64
LANES = 128
WIDE = 256

epsilon = 1e-06


def row_of(vector):
    return vector[...].reshape(1, vector.shape[0])


def wide_of(vector):
    row = row_of(vector)
    return jnp.concatenate([row, jnp.zeros((1, WIDE - C // 2), row.dtype)], axis=-1)


def activated(values, gain_half, keep):
    squares = jnp.sum(values * values, axis=-1, keepdims=True)
    factor = lax.rsqrt(squares * (1.0 / C) + epsilon) * keep
    half = values * factor * gain_half
    return half + half * jnp.tanh(half)


def kept(frame_ok, row, height):
    return jnp.where(frame_ok & (row >= 0) & (row < height), 1.0, 0.0)


def joined(low, high):
    lane = lax.broadcasted_iota(jnp.int32, (low.shape[0], LANES), 1)
    middle = jnp.where(lane < LANES // 2, low[:, LANES:], high[:, :LANES])
    return jnp.concatenate([low[:, :LANES], middle, high[:, LANES:]], axis=-1)


def packed(half, chan):
    return jnp.where(chan == 0, half, pltpu.roll(half, WIDE - C // 2, 1))


def halves(own, other, chan):
    low = jnp.where(chan == 0, own, other)
    high = jnp.where(chan == 0, other, own)
    return joined(low.astype(jnp.float32), high.astype(jnp.float32))


def conv_part(acts, weight, places, frames, rows, col):
    lhs, rhs = [], []
    for depth_at, row_at, frame in places:
        piece = acts[frame : frame + frames, row_at : row_at + rows]
        lhs.append(piece.reshape(frames * rows * LW, C))
        rhs.append(weight[depth_at * 3 + row_at, :, col * C : (col + 1) * C])
    return lax.dot_general(
        jnp.concatenate(lhs, axis=1),
        jnp.concatenate(rhs, axis=1),
        (((1,), (1,)), ((), ())),
        preferred_element_type=jnp.float32,
    )


def columns_summed(parts, span):
    left, here, right = (parts[col, span, :] for col in range(3))
    column = lax.broadcasted_iota(jnp.int32, left.shape, 0)
    left = jnp.where(column == 0, 0.0, pltpu.roll(left, 1, 0))
    right = jnp.where(column == LW - 1, 0.0, pltpu.roll(right, LW - 1, 0))
    return left + here + right


def first_stage(dims, *refs):
    rows_here, height, early, plan = dims
    early_in, early_one, early_two = early
    chunks, refs = list(refs[: len(plan)]), refs[len(plan) :]
    win, bias, gain_in, weight_in, conv_bias_in, second, residual, *refs = refs
    rows, window, pre, acts, parts, own, gain, conv_bias, weight, sems = refs
    fetches = []
    for source, target in (
        (chunks[0], own),
        (gain_in, gain),
        (conv_bias_in, conv_bias),
        (weight_in, weight),
    ):
        fetch = pltpu.make_async_copy(source, target, sems.at[len(fetches)])
        fetch.start()
        fetches.append(fetch)
    space = lax.axis_index("space")
    section = lax.axis_index("tm")
    chan = lax.axis_index("chan")
    row0 = space * rows_here
    groups = LW * ZC // LANES
    lane = lax.broadcasted_iota(jnp.int32, (groups, LANES), 1)
    group = lax.broadcasted_iota(jnp.int32, (groups, LANES), 0)
    low = lane < LANES // 2
    rows_in = rows_here + 8

    fetches[0].wait()
    chunks[0] = own
    for chunk, (back, turn) in zip(chunks, plan):
        count = chunk.shape[0]
        start = early_in // FS * FS * height - back * FS * height
        if turn is not None:
            blocks = FS * height // count
            start = start + lax.rem(space + (blocks - turn), blocks) * count
        values = chunk[...].astype(jnp.float32)
        for at in range(groups):
            rows[pl.ds(start, count), at, :] = values[:, at * LANES : (at + 1) * LANES]

    for frame in range(FS + early_in):
        frame_ok = section * FS - early_in + frame >= 0
        for row in range(rows_in):
            row_abs = row0 - 4 + row
            ok = frame_ok & (row_abs >= 0) & (row_abs < height)
            at = frame * height + jnp.clip(row_abs, 0, height - 1)
            here = jnp.where(ok, rows[at], 0.0)
            before = jnp.where(group == 0, 0.0, pltpu.roll(here, 1, 0))
            after = jnp.where(group == groups - 1, 0.0, pltpu.roll(here, groups - 1, 0))
            for col in range(8):
                source = here
                if col == 0:
                    source = jnp.where(lane >= LANES - ZC, before, here)
                if col == 7:
                    source = jnp.where(lane < ZC, after, here)
                shift = (-ZC * (col - 1)) % LANES
                one = source if shift == 0 else pltpu.roll(source, shift, 1)
                two = pltpu.roll(source, (shift + LANES // 2) % LANES, 1)
                window.at[frame, row][pl.ds(col, groups, stride=8), :] = jnp.where(low, one, two)

    rows_one = rows_here + 6
    rows_two = rows_here + 4
    lane_wide = lax.broadcasted_iota(jnp.int32, (rows_one, LW, LANES), 2)

    def input_conv(frame):
        slots = []
        for depth_at in (2, 1, 0):
            source = frame - early_one - 2 + depth_at + early_in
            if source >= 0:
                slots += [(source, row_at) for row_at in range(3)]
        pieces = []
        for pair in range(0, len(slots), 2):
            source, row_at = slots[pair]
            value = window[source, row_at : row_at + rows_one]
            second_slot = 0.0
            if pair + 1 < len(slots):
                source, row_at = slots[pair + 1]
                second_slot = window[source, row_at : row_at + rows_one]
            value = jnp.where(lane_wide < LANES // 2, value, second_slot)
            pieces.append(value.astype(jnp.bfloat16).reshape(rows_one * LW, LANES))
        lhs = jnp.concatenate(pieces, axis=-1)
        pre[frame % 2] = jnp.dot(
            lhs, win[0 : lhs.shape[1]], preferred_element_type=jnp.float32
        )

    def activate(frame, row):
        frame_ok = section * FS - early_one + frame >= 0
        out = pre[frame % 2, row * LW : (row + 1) * LW] + bias[...]
        out = out.astype(jnp.bfloat16).astype(jnp.float32)
        if frame >= early_one and 2 <= row < rows_one - 2:
            mine = jnp.where(chan == 0, out[:, :WIDE], pltpu.roll(out[:, LANES:], C // 2, 1))
            span = pl.ds((row - 2) * LW, LW)
            residual[frame - early_one, span, :] = mine.astype(jnp.bfloat16)
        keep = kept(frame_ok, row0 - 3 + row, height)
        act = activated(out, row_of(gain) * 0.5, keep)
        acts[frame, row] = act.astype(jnp.bfloat16)

    def convolve(frame, col):
        places = []
        for depth_at in (2, 1, 0):
            source = frame - early_two - 2 + depth_at + early_one
            if source >= 0:
                places += [(depth_at, row_at, source) for row_at in range(3)]
        product = conv_part(acts, weight, places, 1, rows_two, col)
        parts[frame % 2, col, :, 0 : C // 2] = product

    def finish(frame):
        for row in range(rows_two):
            total = columns_summed(parts.at[frame % 2], pl.ds(row * LW, LW))
            total = packed(total + wide_of(conv_bias), chan)
            span = pl.ds((frame * rows_two + row) * LW, LW)
            second[span, :] = total.astype(jnp.bfloat16)

    lead = early_one - early_two
    frames_one = FS + early_one
    fetches[1].wait()
    fetches[2].wait()
    for frame in range(lead + 1):
        input_conv(frame)
        for row in range(rows_one):
            activate(frame, row)
    fetches[3].wait()
    for frame in range(FS + early_two):
        later = frame + lead + 1
        row = 0
        if later < frames_one:
            input_conv(later)
        for col in range(3):
            convolve(frame, col)
            while later < frames_one and row * 3 < rows_one * (col + 1):
                activate(later, row)
                row += 1
        finish(frame)


def second_stage(dims, own, other, residual, gain, weight, conv_bias, block, acts, parts):
    rows_here, height, early_two = dims
    section = lax.axis_index("tm")
    chan = lax.axis_index("chan")
    row0 = lax.axis_index("space") * rows_here
    rows_two = rows_here + 4
    rows_three = rows_here + 2
    frames_two = FS + early_two

    def activate(frame):
        frame_ok = section * FS - early_two + frame >= 0
        half_gain = row_of(gain) * 0.5
        for row in range(rows_two):
            span = pl.ds((frame * rows_two + row) * LW, LW)
            values = halves(own[span, :], other[span, :], chan)
            act = activated(values, half_gain, kept(frame_ok, row0 - 2 + row, height))
            acts[frame, row] = act.astype(jnp.bfloat16)

    done = 0
    first = True
    for depth_at in range(3):
        skip = max(0, 2 - early_two - depth_at)
        count = FS - skip
        if count <= 0:
            continue
        start = skip - 2 + depth_at + early_two
        while done < start + count:
            activate(done)
            done += 1
        places = [(depth_at, row_at, start) for row_at in range(3)]
        from_row = skip * rows_three * LW
        for col in range(3):
            product = conv_part(acts, weight, places, count, rows_three, col)
            if first:
                if from_row:
                    parts[col, 0:from_row, :] = jnp.zeros((from_row, WIDE), jnp.float32)
                parts[col, from_row:, 0 : C // 2] = product
            else:
                parts[col, from_row:, 0 : C // 2] += product
        first = False
    for row in range(FS * rows_three):
        span = pl.ds(row * LW, LW)
        total = columns_summed(parts, span) + wide_of(conv_bias)
        total = total + residual[span, :].astype(jnp.float32)
        block[span, :] = packed(total, chan).astype(jnp.bfloat16)


def third_stage(dims, own, other, weight, up_bias, decoded, acts, raw):
    rows_here, height = dims
    chan = lax.axis_index("chan")
    row0 = lax.axis_index("space") * rows_here
    rows_three = rows_here + 2
    out_chan = weight.shape[1] // 4
    for frame in range(FS):
        for row in range(rows_three):
            span = pl.ds((frame * rows_three + row) * LW, LW)
            values = halves(own[span, :], other[span, :], chan)
            values = values * kept(True, row0 - 1 + row, height)
            acts[frame, row] = values.astype(jnp.bfloat16)
    count = FS * rows_here * LW
    source = lax.broadcasted_iota(jnp.int32, (4 * LW, 4 * LW), 0)
    target = lax.broadcasted_iota(jnp.int32, (4 * LW, 4 * LW), 1)
    phase = source // (2 * LW)
    place = source % (2 * LW)
    wanted = (place // LW) * (2 * LW) + (place % LW) * 2 + phase
    shuffle = jnp.where(wanted == target, 1.0, 0.0).astype(jnp.bfloat16)
    column_bias = row_of(up_bias).T
    column = lax.broadcasted_iota(jnp.int32, (out_chan, 2 * LW), 1) % LW
    for row_phase in range(2):
        lhs = [
            acts[:, at : at + rows_here].reshape(count, C)
            for at in (row_phase, row_phase + 1)
        ]
        raw[row_phase] = lax.dot_general(
            weight[row_phase],
            jnp.concatenate(lhs, axis=1),
            (((1,), (1,)), ((), ())),
            preferred_element_type=jnp.float32,
        )
        pairs = []
        for start in range(0, count, 2 * LW):
            left, even, odd, right = (
                raw[row_phase, at * out_chan : (at + 1) * out_chan, start : start + 2 * LW]
                for at in range(4)
            )
            left = jnp.where(column == 0, 0.0, pltpu.roll(left, 1, 1))
            right = jnp.where(column == LW - 1, 0.0, pltpu.roll(right, 2 * LW - 1, 1))
            pair = jnp.concatenate([left + even + column_bias, odd + right + column_bias], axis=1)
            pairs.append(pair.astype(jnp.bfloat16))
        pixels = jnp.dot(
            jnp.concatenate(pairs, axis=0), shuffle, preferred_element_type=jnp.float32
        ).astype(jnp.bfloat16)
        for at in range(len(pairs)):
            frame, row = divmod(2 * at, rows_here)
            part = pixels[at * out_chan : (at + 1) * out_chan]
            decoded[frame, 2 * row + row_phase] = part[:, : 2 * LW]
            decoded[frame, 2 * row + 2 + row_phase] = part[:, 2 * LW :]


def prepare(own_in, other_in, own_bias, other_bias, up_in, win, bias, phases, own, own_b, up, sems):
    fetches = []
    for source, target in ((own_in, own), (own_bias, own_b), (up_in, up)):
        fetch = pltpu.make_async_copy(source, target, sems.at[len(fetches)])
        fetch.start()
        fetches.append(fetch)
    chan = lax.axis_index("chan")
    fetches[0].wait()
    fetches[1].wait()
    mine, other = own[...].astype(jnp.float32), other_in[...].astype(jnp.float32)
    low = jnp.where(chan == 0, mine, other)
    high = jnp.where(chan == 0, other, mine)
    joint = jnp.concatenate([low, high], axis=0).T.astype(jnp.bfloat16)
    blank = jnp.zeros((LANES // 2, C), jnp.bfloat16)
    for slot in range(10):
        win[slot * 64 : slot * 64 + 64, :] = blank
    for slot in range(9):
        source = ((2 - slot // 3) * 3 + slot % 3) * 3 * ZC
        win[slot * 64 : slot * 64 + 3 * ZC, :] = joint[source : source + 3 * ZC]
    mine_b, other_b = row_of(own_b), row_of(other_bias)
    low = jnp.where(chan == 0, mine_b, other_b)
    high = jnp.where(chan == 0, other_b, mine_b)
    bias[...] = jnp.concatenate([low, high], axis=1)
    fetches[2].wait()
    count = up.shape[1]
    for row_phase, split in enumerate((((0,), (1, 2)), ((0, 1), (2,)))):
        for row_at, taps in enumerate(split):
            cols = []
            for c in range(3):
                cut = pl.ds(c * C, C)
                value = up[taps[0], :, cut].astype(jnp.float32)
                for tap in taps[1:]:
                    value = value + up[tap, :, cut].astype(jnp.float32)
                cols.append(value)
            grouped = (cols[0], cols[1] + cols[2], cols[0] + cols[1], cols[2])
            for at, value in enumerate(grouped):
                target = (row_phase, pl.ds(at * count, count), pl.ds(row_at * C, C))
                phases[target] = value.astype(jnp.bfloat16)


def limits(mib):
    return pltpu.CompilerParams(vmem_limit_bytes=mib * 1024 * 1024)


def shards(
    latent,
    in_weight,
    in_bias,
    first_gain,
    first_weight,
    first_bias,
    second_gain,
    second_weight,
    second_bias,
    up_weight,
    up_bias,
):
    space_count = lax.axis_size("space")
    tm_count = lax.axis_size("tm")
    rows_here = latent.shape[1] // FS
    height = rows_here * space_count
    groups = LW * ZC // LANES
    earlier = FS * (tm_count - 1)
    early_two, early_one, early_in = min(2, earlier), min(4, earlier), min(6, earlier)
    swap = [(0, 1), (1, 0)]

    plan = []
    if space_count <= 4:
        section_chunks = [latent[0]]
        for turn in range(1, space_count):
            pairs = [(i, (i + turn) % space_count) for i in range(space_count)]
            section_chunks.append(lax.ppermute(latent[0], "space", pairs))
        turns = list(range(space_count))
    else:
        section_chunks = [lax.all_gather(latent[0], "space", axis=0, tiled=True)]
        turns = [None]
    chunks = list(section_chunks)
    plan = [(0, turn) for turn in turns]
    for back in range(1, early_in // FS + 1):
        pairs = [(i, (i + back) % tm_count) for i in range(tm_count)]
        for chunk, turn in zip(section_chunks, turns):
            chunks.append(lax.ppermute(chunk, "tm", pairs))
            plan.append((back, turn))

    stored_in = jnp.swapaxes(in_weight, 0, 1)
    stored_up = jnp.swapaxes(up_weight, 1, 2)
    out_chan = up_weight.shape[-1]
    def stay(array):
        return pltpu.with_memory_space_constraint(array, pltpu.HBM)

    vmem, hbm = pl.BlockSpec(memory_space=pltpu.VMEM), pl.BlockSpec(memory_space=pltpu.HBM)
    win, bias, phases = pl.pallas_call(
        prepare,
        out_shape=(
            jax.ShapeDtypeStruct((5 * LANES, C), jnp.bfloat16),
            jax.ShapeDtypeStruct((1, C), jnp.float32),
            jax.ShapeDtypeStruct((2, 4 * out_chan, 2 * C), jnp.bfloat16),
        ),
        in_specs=[hbm, vmem, hbm, vmem, hbm],
        out_specs=(vmem,) * 3,
        scratch_shapes=[
            pltpu.VMEM(stored_in.shape, jnp.bfloat16),
            pltpu.VMEM(in_bias.shape, jnp.float32),
            pltpu.VMEM(stored_up.shape, jnp.bfloat16),
            pltpu.SemaphoreType.DMA((3,)),
        ],
        compiler_params=limits(12),
        name="prepare",
    )(
        stay(stored_in),
        lax.ppermute(stored_in, "chan", swap),
        stay(in_bias),
        lax.ppermute(in_bias, "chan", swap),
        stay(stored_up),
    )

    voxels_two = (FS + early_two) * (rows_here + 4) * LW
    voxels_three = FS * (rows_here + 2) * LW
    early = (early_in, early_one, early_two)
    stored_first = jnp.swapaxes(first_weight, 1, 2)
    second_own, residual = pl.pallas_call(
        functools.partial(first_stage, (rows_here, height, early, tuple(plan))),
        out_shape=(
            jax.ShapeDtypeStruct((voxels_two, WIDE), jnp.bfloat16),
            jax.ShapeDtypeStruct((FS, (rows_here + 2) * LW, WIDE), jnp.bfloat16),
        ),
        in_specs=[hbm] + [vmem] * (len(chunks) + 1) + [hbm] * 3,
        out_specs=(vmem,) * 2,
        scratch_shapes=[
            pltpu.VMEM(((FS + early_in) * height, groups, LANES), jnp.float32),
            pltpu.VMEM((FS + early_in, rows_here + 8, LW, LANES), jnp.float32),
            pltpu.VMEM((2, (rows_here + 6) * LW, C), jnp.float32),
            pltpu.VMEM((FS + early_one, rows_here + 6, LW, C), jnp.bfloat16),
            pltpu.VMEM((2, 3, (rows_here + 4) * LW, WIDE), jnp.float32),
            pltpu.VMEM(chunks[0].shape, jnp.bfloat16),
            pltpu.VMEM(first_gain.shape, jnp.float32),
            pltpu.VMEM(first_bias.shape, jnp.float32),
            pltpu.VMEM(stored_first.shape, jnp.bfloat16),
            pltpu.SemaphoreType.DMA((4,)),
        ],
        compiler_params=limits(28),
        name="first_stage",
    )(
        stay(chunks[0]),
        *chunks[1:],
        win,
        bias,
        stay(first_gain),
        stay(stored_first),
        stay(first_bias),
    )
    second_other = lax.ppermute(second_own, "chan", swap)

    block_own = pl.pallas_call(
        functools.partial(second_stage, (rows_here, height, early_two)),
        out_shape=jax.ShapeDtypeStruct((voxels_three, WIDE), jnp.bfloat16),
        in_specs=[vmem] * 6,
        out_specs=vmem,
        scratch_shapes=[
            pltpu.VMEM((FS + early_two, rows_here + 4, LW, C), jnp.bfloat16),
            pltpu.VMEM((3, voxels_three, WIDE), jnp.float32),
        ],
        compiler_params=limits(16),
        name="second_stage",
    )(
        second_own,
        second_other,
        residual.reshape(voxels_three, WIDE),
        second_gain,
        jnp.swapaxes(second_weight, 1, 2),
        second_bias,
    )
    block_other = lax.ppermute(block_own, "chan", swap)

    return pl.pallas_call(
        functools.partial(third_stage, (rows_here, height)),
        out_shape=jax.ShapeDtypeStruct((FS, 2 * rows_here, out_chan, 2 * LW), jnp.bfloat16),
        in_specs=[vmem] * 4,
        out_specs=vmem,
        scratch_shapes=[
            pltpu.VMEM((FS, rows_here + 2, LW, C), jnp.bfloat16),
            pltpu.VMEM((2, 4 * out_chan, FS * rows_here * LW), jnp.float32),
        ],
        compiler_params=limits(12),
        name="third_stage",
    )(block_own, block_other, phases, up_bias)


def solution(mesh):
    placed = (
        P(("groups", "tm"), "space", None),
        P(None, "chan"),
        P("chan"),
        P(),
        P(None, None, "chan"),
        P("chan"),
        P(),
        P(None, None, "chan"),
        P("chan"),
        P(None, None, "chan"),
        P("chan"),
    )
    return jax.shard_map(
        shards,
        mesh=mesh,
        in_specs=placed,
        out_specs=P(("groups", "tm"), "space", "chan", None),
        check_vma=False,
    )
```

time: 50 us -> 35.2 us (0.70)
  local copies, waits for them, and re-layouts: 8.66 us -> 0.02 us
  Pallas kernels: 25.2 us -> 17.4 us
  other arithmetic: 3.95 us -> 0 us
  waiting for transfers between devices: 3.68 us -> 6.65 us
  starting transfers between devices: 8.08 us -> 10.9 us
    ppermute x2 -> x9, starting transfers between devices: 0.64 us -> 10.6 us  [the longest x3 5.66 us: shards(): section_chunks.append(lax.ppermute(latent[0], 'space', pairs))]
    all_to_all x1 -> x0, starting transfers between devices: 7.22 us -> none  [shards(): lat = lax.all_to_all(piece, ('tm', 'space'), 0, 0, tiled=True)]
    pallas_call x2 -> x3, Pallas kernels: 20.9 us -> 15.4 us  [the longest x1 10.2 us: shards(): pl.pallas_call(functools.partial(first_stage, (rows_here, height, early,...]
    all_to_all x1 -> x0, waiting for transfers between devices: 3.37 us -> none  [shards(): lat = lax.all_to_all(piece, ('tm', 'space'), 0, 0, tiled=True)]
    unnamed x19 -> x8, local copies, waits for them, and re-layouts: 3.34 us -> 0.02 us
    ppermute x2 -> x9, waiting for transfers between devices: 0.01 us -> 2.97 us  [the longest x1 1.37 us: shards(): lax.ppermute(in_bias, 'chan', swap)]
    pallas_call x1, Pallas kernels: 4.21 us -> 1.95 us  [shards(): pl.pallas_call(functools.partial(third_stage, (rows_here, height)), out_s...]
    pad x3 -> x0, local copies, waits for them, and re-layouts: 2.02 us -> none  [the longest x2 1.17 us: wide(): return jnp.pad(vector, (0, WIDE - half)).reshape(1, WIDE)]
  transfers between devices with their start and end apart: 5 -> 11, of which waited for: 2 -> 5; matrix products, arithmetic and copies ran while one was open for 19% -> 0% of each run, Pallas kernels for 0% -> 4%
where the time goes in v2:
time: 35.2 us; the launch traced here: 35 us
  Pallas kernels  17.4 us (49%)
  starting transfers between devices  10.9 us (31%)
  waiting for transfers between devices  6.65 us (19%)
    pallas_call x1, Pallas kernels, shards(): pl.pallas_call(functools.partial(first_stage, (rows_here, height, early,...  10.2 us
    ppermute x3, starting transfers between devices, shards(): section_chunks.append(lax.ppermute(latent[0], 'space', pairs))  5.66 us
    ppermute x4, starting transfers between devices, shards(): chunks.append(lax.ppermute(chunk, 'tm', pairs))  4.42 us
    pallas_call x1, Pallas kernels, shards(): pl.pallas_call(functools.partial(second_stage, (rows_here, height, early_...  3.72 us
    ppermute x1, waiting for transfers between devices, shards(): second_other = lax.ppermute(second_own, 'chan', swap)  2.27 us
    pallas_call x1, Pallas kernels, shards(): pl.pallas_call(functools.partial(third_stage, (rows_here, height)), out_s...  1.95 us
    pallas_call x1, Pallas kernels, shards(): pl.pallas_call(prepare, out_shape=(jax.ShapeDtypeStruct((5 * LANES, C), j...  1.47 us
    ppermute x1, waiting for transfers between devices, shards(): block_other = lax.ppermute(block_own, 'chan', swap)  1.41 us
  transfers between devices with their start and end apart: 11, of which 5 were waited for; matrix products, arithmetic and copies ran while one was open for 0% of the time, Pallas kernels for 4%

profile of v2, /device:TPU:0, one launch (start us, length us, event | category | flops | bytes accessed | tf_op | source)
XLA Modules:
  0.0 35.0 jit_solution(9859536216546152056)
XLA Ops:
  0.0 0.6 %collective-permute-start.7 = (bf16[192,432]{1,0:T(8,128)(2,1)}, bf16[192,432]{1,0:T(8,128)(2,1)S(1)}, u32[]{:S(2)}, u32[]{:S(2)}) collective-permute-start(bf16[192,432]{1,0:T(8,128)(2,1)} %bitcast.10), channel_id=1, source_target_pairs={{0,1},{1,0},{2,3},{3,2},{4,5},{5,4},{6,7},{7,6},{8,9},{9,8},{10,11... | collective-permute-start | bytes 497672 | tf_op jit(solution)/shard_map/ppermute | solution.py:420
  0.6 4.7 %collective-permute-start.2 = (bf16[4,1024]{1,0:T(4,128)(2,1)}, bf16[4,1024]{1,0:T(4,128)(2,1)S(1)}, u32[]{:S(2)}, u32[]{:S(2)}) collective-permute-start(bf16[4,1024]{1,0:T(4,128)(2,1)} %bitcast.12), channel_id=1, source_target_pairs={{0,12},{4,0},{8,4},{12,8},{1,13},{5,1},{9,5},{13,9},{2,14},{6,2},{... | collective-permute-start | bytes 24584 | tf_op jit(solution)/shard_map/ppermute | solution.py:381
  5.2 0.0 collective-permute-start.1
  5.2 1.0 %collective-permute-start = (bf16[4,1024]{1,0:T(4,128)(2,1)}, bf16[4,1024]{1,0:T(4,128)(2,1)S(1)}, u32[]{:S(2)}, u32[]{:S(2)}) collective-permute-start(bf16[4,1024]{1,0:T(4,128)(2,1)} %bitcast.14), channel_id=1, source_target_pairs={{0,4},{4,8},{8,12},{12,0},{1,5},{5,9},{9,13},{13,1},{2,6},{6,10},{... | collective-permute-start | bytes 24584 | tf_op jit(solution)/shard_map/ppermute | solution.py:381
  6.2 0.0 collective-permute-start.8
  6.2 1.4 %collective-permute-done.8.other_bias = f32[192]{0:T(256)S(1)} collective-permute-done((f32[192]{0:T(256)}, f32[192]{0:T(256)S(1)}, u32[]{:S(2)}, u32[]{:S(2)}) %collective-permute-start.8) | collective-permute-done | bytes 800 | tf_op jit(solution)/shard_map/ppermute | solution.py:422
  7.6 1.5 %collective-permute-start.3 = (bf16[4,1024]{1,0:T(4,128)(2,1)}, bf16[4,1024]{1,0:T(4,128)(2,1)S(1)}, u32[]{:S(2)}, u32[]{:S(2)}) collective-permute-start(bf16[4,1024]{1,0:T(4,128)(2,1)} %bitcast.15), channel_id=1, source_target_pairs={{0,2},{2,0},{1,3},{3,1},{4,6},{6,4},{5,7},{7,5},{8,10},{10,8},{9,1... | collective-permute-start | bytes 24584 | tf_op jit(solution)/shard_map/ppermute | solution.py:391
  9.1 0.0 collective-permute-done.2.refs_3_
  9.1 0.5 %collective-permute-start.6 = (bf16[4,1024]{1,0:T(4,128)(2,1)S(1)}, bf16[4,1024]{1,0:T(4,128)(2,1)S(1)}, u32[]{:S(2)}, u32[]{:S(2)}) collective-permute-start(bf16[4,1024]{1,0:T(4,128)(2,1)S(1)} %collective-permute-done.2.refs_3_), channel_id=1, source_target_pairs={{0,2},{2,0},{1,3},{3,1},{4,6},{6,4},{5,7},{7,5},{8,10},{10,8},{9,1... | collective-permute-start | bytes 24584 | tf_op jit(solution)/shard_map/ppermute | solution.py:391
  9.6 0.3 collective-permute-done.1.refs_2_
  10.0 1.5 %collective-permute-start.5 = (bf16[4,1024]{1,0:T(4,128)(2,1)S(1)}, bf16[4,1024]{1,0:T(4,128)(2,1)S(1)}, u32[]{:S(2)}, u32[]{:S(2)}) collective-permute-start(bf16[4,1024]{1,0:T(4,128)(2,1)S(1)} %collective-permute-done.1.refs_2_), channel_id=1, source_target_pairs={{0,2},{2,0},{1,3},{3,1},{4,6},{6,4},{5,7},{7,5},{8,10},{10,8},{9,1... | collective-permute-start | bytes 24584 | tf_op jit(solution)/shard_map/ppermute | solution.py:391
  11.5 0.9 %collective-permute-start.4 = (bf16[4,1024]{1,0:T(4,128)(2,1)S(1)}, bf16[4,1024]{1,0:T(4,128)(2,1)S(1)}, u32[]{:S(2)}, u32[]{:S(2)}) collective-permute-start(bf16[4,1024]{1,0:T(4,128)(2,1)S(1)} %collective-permute-done.refs_1_), channel_id=1, source_target_pairs={{0,2},{2,0},{1,3},{3,1},{4,6},{6,4},{5,7},{7,5},{8,10},{10,8},{9,1... | collective-permute-start | bytes 24584 | tf_op jit(solution)/shard_map/ppermute | solution.py:391
  12.4 1.5 %prepare.1 = (bf16[640,384]{1,0:T(8,128)(2,1)S(1)}, f32[1,384]{1,0:T(1,128)S(1)}, bf16[2,384,768]{2,1,0:T(8,128)(2,1)S(1)}) custom-call(bf16[192,432]{1,0:T(8,128)(2,1)} %bitcast.11, bf16[192,432]{1,0:T(8,128)(2,1)S(1)} %collective-permute-done.7.other_in, f32[192]{0:T(256)} %own_bias.1, f32[192]{0:T(256)S(1)} %collective-permute-done.8.other_bias, ...), custom_call_target="tpu_custom_call" | custom-call | tf_op jit(solution)/shard_map/prepare/pallas_call | solution.py:401
  13.9 0.0 collective-permute-done.6.refs_7_
  13.9 0.0 collective-permute-done.5.refs_6_
  13.9 1.2 %collective-permute-done.4.refs_5_ = bf16[4,1024]{1,0:T(4,128)(2,1)S(1)} collective-permute-done((bf16[4,1024]{1,0:T(4,128)(2,1)S(1)}, bf16[4,1024]{1,0:T(4,128)(2,1)S(1)}, u32[]{:S(2)}, u32[]{:S(2)}) %collective-permute-start.4) | collective-permute-done | bytes 8224 | tf_op jit(solution)/shard_map/ppermute | solution.py:391
  15.1 10.2 %first_stage.1 = (bf16[1536,256]{1,0:T(8,128)(2,1)S(1)}, bf16[2,256,256]{2,1,0:T(8,128)(2,1)S(1)}) custom-call(bf16[4,1024]{1,0:T(4,128)(2,1)} %bitcast.16, bf16[4,1024]{1,0:T(4,128)(2,1)S(1)} %collective-permute-done.refs_1_, bf16[4,1024]{1,0:T(4,128)(2,1)S(1)} %collective-permute-done.1.refs_2_, bf16[4,1024]{1,0:T(4,128)(2,1)S(1)} %collective-permute-done.2.refs_3_, ...), custom_call_target="tpu_custom_call" | custom-call | tf_op jit(solution)/shard_map/first_stage/pallas_call | solution.py:430
  25.4 0.0 copy-start.3
  25.4 0.1 collective-permute-start.9
  25.4 2.3 %collective-permute-done.9.other = bf16[1536,256]{1,0:T(8,128)(2,1)S(1)} collective-permute-done((bf16[1536,256]{1,0:T(8,128)(2,1)S(1)}, bf16[1536,256]{1,0:T(8,128)(2,1)S(1)}, u32[]{:S(2)}, u32[]{:S(2)}) %collective-permute-start.9) | collective-permute-done | bytes 786464 | tf_op jit(solution)/shard_map/ppermute | solution.py:461
  27.7 3.7 %second_stage.1.own = bf16[512,256]{1,0:T(8,128)(2,1)S(1)} custom-call(bf16[1536,256]{1,0:T(8,128)(2,1)S(1)} %get-tuple-element.12.own, bf16[1536,256]{1,0:T(8,128)(2,1)S(1)} %collective-permute-done.9.other, bf16[512,256]{1,0:T(8,128)(2,1)S(1)} %bitcast.7, f32[384]{0:T(512)S(1)} %copy-done.1, bf16[9,192,1152]{2,1,0:T(8,128)(2,1)S(1)} %bitcast.6, ...), custom_call_target="tpu_custom_call" | custom-call | tf_op jit(solution)/shard_map/second_stage/pallas_call | solution.py:463
  31.5 0.2 collective-permute-start.10
  31.6 1.4 %collective-permute-done.10.other = bf16[512,256]{1,0:T(8,128)(2,1)S(1)} collective-permute-done((bf16[512,256]{1,0:T(8,128)(2,1)S(1)}, bf16[512,256]{1,0:T(8,128)(2,1)S(1)}, u32[]{:S(2)}, u32[]{:S(2)}) %collective-permute-start.10) | collective-permute-done | bytes 262176 | tf_op jit(solution)/shard_map/ppermute | solution.py:482
  33.1 1.9 %third_stage.1 = bf16[2,4,96,128]{3,2,1,0:T(8,128)(2,1)} custom-call(bf16[512,256]{1,0:T(8,128)(2,1)S(1)} %second_stage.1.own, bf16[512,256]{1,0:T(8,128)(2,1)S(1)} %collective-permute-done.10.other, bf16[2,384,768]{2,1,0:T(8,128)(2,1)S(1)} %get-tuple-element.14.weight, f32[96]{0:T(128)S(1)} %copy-done.3), custom_call_target="tpu_custom_call" | custom-call | tf_op jit(solution)/shard_map/third_stage/pallas_call | solution.py:484
  (10 shorter events, 0.0 us)
Async XLA Ops:
  0.0 27.7 %copy-start.2 = (f32[192]{0:T(256)S(1)}, f32[192]{0:T(256)}, u32[]{:S(2)}) copy-start(f32[192]{0:T(256)} %conv_bias.1) | copy-start | bytes 2308
  0.0 27.7 %copy-start = (bf16[9,1152,192]{1,2,0:T(8,128)(2,1)S(1)}, bf16[9,1152,192]{1,2,0:T(8,128)(2,1)}, u32[]{:S(2)}) copy-start(bf16[9,1152,192]{1,2,0:T(8,128)(2,1)} %param.18) | copy-start | bytes 11943940
  0.0 27.7 %copy-start.1 = (f32[384]{0:T(512)S(1)}, f32[384]{0:T(512)}, u32[]{:S(2)}) copy-start(f32[384]{0:T(512)} %gain.1) | copy-start | bytes 4612
  0.0 12.4 %collective-permute-start.7 = (bf16[192,432]{1,0:T(8,128)(2,1)}, bf16[192,432]{1,0:T(8,128)(2,1)S(1)}, u32[]{:S(2)}, u32[]{:S(2)}) collective-permute-start(bf16[192,432]{1,0:T(8,128)(2,1)} %bitcast.10), channel_id=1, source_target_pairs={{0,1},{1,0},{2,3},{3,2},{4,5},{5,4},{6,7},{7,6},{8,9},{9,8},{10,11... | collective-permute-start | bytes 497672 | tf_op jit(solution)/shard_map/ppermute | solution.py:420
  0.6 8.5 %collective-permute-start.2 = (bf16[4,1024]{1,0:T(4,128)(2,1)}, bf16[4,1024]{1,0:T(4,128)(2,1)S(1)}, u32[]{:S(2)}, u32[]{:S(2)}) collective-permute-start(bf16[4,1024]{1,0:T(4,128)(2,1)} %bitcast.12), channel_id=1, source_target_pairs={{0,12},{4,0},{8,4},{12,8},{1,13},{5,1},{9,5},{13,9},{2,14},{6,2},{... | collective-permute-start | bytes 24584 | tf_op jit(solution)/shard_map/ppermute | solution.py:381
  5.2 4.8 %collective-permute-start.1 = (bf16[4,1024]{1,0:T(4,128)(2,1)}, bf16[4,1024]{1,0:T(4,128)(2,1)S(1)}, u32[]{:S(2)}, u32[]{:S(2)}) collective-permute-start(bf16[4,1024]{1,0:T(4,128)(2,1)} %bitcast.13), channel_id=1, source_target_pairs={{0,8},{4,12},{8,0},{12,4},{1,9},{5,13},{9,1},{13,5},{2,10},{6,14},... | collective-permute-start | bytes 24584 | tf_op jit(solution)/shard_map/ppermute | solution.py:381
  5.2 6.3 %collective-permute-start = (bf16[4,1024]{1,0:T(4,128)(2,1)}, bf16[4,1024]{1,0:T(4,128)(2,1)S(1)}, u32[]{:S(2)}, u32[]{:S(2)}) collective-permute-start(bf16[4,1024]{1,0:T(4,128)(2,1)} %bitcast.14), channel_id=1, source_target_pairs={{0,4},{4,8},{8,12},{12,0},{1,5},{5,9},{9,13},{13,1},{2,6},{6,10},{... | collective-permute-start | bytes 24584 | tf_op jit(solution)/shard_map/ppermute | solution.py:381
  6.2 1.4 %collective-permute-start.8 = (f32[192]{0:T(256)}, f32[192]{0:T(256)S(1)}, u32[]{:S(2)}, u32[]{:S(2)}) collective-permute-start(f32[192]{0:T(256)} %own_bias.1), channel_id=1, source_target_pairs={{0,1},{1,0},{2,3},{3,2},{4,5},{5,4},{6,7},{7,6},{8,9},{9,8},{10,11... | collective-permute-start | bytes 2312 | tf_op jit(solution)/shard_map/ppermute | solution.py:422
  7.6 6.2 %collective-permute-start.3 = (bf16[4,1024]{1,0:T(4,128)(2,1)}, bf16[4,1024]{1,0:T(4,128)(2,1)S(1)}, u32[]{:S(2)}, u32[]{:S(2)}) collective-permute-start(bf16[4,1024]{1,0:T(4,128)(2,1)} %bitcast.15), channel_id=1, source_target_pairs={{0,2},{2,0},{1,3},{3,1},{4,6},{6,4},{5,7},{7,5},{8,10},{10,8},{9,1... | collective-permute-start | bytes 24584 | tf_op jit(solution)/shard_map/ppermute | solution.py:391
  9.1 4.8 %collective-permute-start.6 = (bf16[4,1024]{1,0:T(4,128)(2,1)S(1)}, bf16[4,1024]{1,0:T(4,128)(2,1)S(1)}, u32[]{:S(2)}, u32[]{:S(2)}) collective-permute-start(bf16[4,1024]{1,0:T(4,128)(2,1)S(1)} %collective-permute-done.2.refs_3_), channel_id=1, source_target_pairs={{0,2},{2,0},{1,3},{3,1},{4,6},{6,4},{5,7},{7,5},{8,10},{10,8},{9,1... | collective-permute-start | bytes 24584 | tf_op jit(solution)/shard_map/ppermute | solution.py:391
  10.0 3.9 %collective-permute-start.5 = (bf16[4,1024]{1,0:T(4,128)(2,1)S(1)}, bf16[4,1024]{1,0:T(4,128)(2,1)S(1)}, u32[]{:S(2)}, u32[]{:S(2)}) collective-permute-start(bf16[4,1024]{1,0:T(4,128)(2,1)S(1)} %collective-permute-done.1.refs_2_), channel_id=1, source_target_pairs={{0,2},{2,0},{1,3},{3,1},{4,6},{6,4},{5,7},{7,5},{8,10},{10,8},{9,1... | collective-permute-start | bytes 24584 | tf_op jit(solution)/shard_map/ppermute | solution.py:391
  11.5 3.7 %collective-permute-start.4 = (bf16[4,1024]{1,0:T(4,128)(2,1)S(1)}, bf16[4,1024]{1,0:T(4,128)(2,1)S(1)}, u32[]{:S(2)}, u32[]{:S(2)}) collective-permute-start(bf16[4,1024]{1,0:T(4,128)(2,1)S(1)} %collective-permute-done.refs_1_), channel_id=1, source_target_pairs={{0,2},{2,0},{1,3},{3,1},{4,6},{6,4},{5,7},{7,5},{8,10},{10,8},{9,1... | collective-permute-start | bytes 24584 | tf_op jit(solution)/shard_map/ppermute | solution.py:391
  25.4 7.7 %copy-start.3 = (f32[96]{0:T(128)S(1)}, f32[96]{0:T(128)}, u32[]{:S(2)}) copy-start(f32[96]{0:T(128)} %up_bias.1) | copy-start | bytes 1156
  25.4 2.4 %collective-permute-start.9 = (bf16[1536,256]{1,0:T(8,128)(2,1)S(1)}, bf16[1536,256]{1,0:T(8,128)(2,1)S(1)}, u32[]{:S(2)}, u32[]{:S(2)}) collective-permute-start(bf16[1536,256]{1,0:T(8,128)(2,1)S(1)} %get-tuple-element.12.own), channel_id=1, source_target_pairs={{0,1},{1,0},{2,3},{3,2},{4,5},{5,4},{6,7},{7,6},{8,9},{9,8},{10,11... | collective-permute-start | bytes 2359304 | tf_op jit(solution)/shard_map/ppermute | solution.py:461
  31.5 1.6 %collective-permute-start.10 = (bf16[512,256]{1,0:T(8,128)(2,1)S(1)}, bf16[512,256]{1,0:T(8,128)(2,1)S(1)}, u32[]{:S(2)}, u32[]{:S(2)}) collective-permute-start(bf16[512,256]{1,0:T(8,128)(2,1)S(1)} %second_stage.1.own), channel_id=1, source_target_pairs={{0,1},{1,0},{2,3},{3,2},{4,5},{5,4},{6,7},{7,6},{8,9},{9,8},{10,11... | collective-permute-start | bytes 786440 | tf_op jit(solution)/shard_map/ppermute | solution.py:482

commit v3 on v2

v3 whole, which is shorter than its diff:
```python
import functools

import jax
import jax.numpy as jnp
from jax import lax
from jax.experimental import pallas as pl
from jax.experimental.pallas import tpu as pltpu
from jax.sharding import PartitionSpec as P

ZC = 16
C = 384
FS = 2
LW = 64
LANES = 128
WIDE = 256

epsilon = 1e-06


def row_of(vector):
    return vector[...].reshape(1, vector.shape[0])


def wide_of(vector):
    row = row_of(vector)
    return jnp.concatenate([row, jnp.zeros((1, WIDE - C // 2), row.dtype)], axis=-1)


def activated(values, gain_half, keep):
    squares = jnp.sum(values * values, axis=-1, keepdims=True)
    factor = lax.rsqrt(squares * (1.0 / C) + epsilon) * keep
    half = values * factor * gain_half
    return half + half * jnp.tanh(half)


def kept(frame_ok, row, height):
    return jnp.where(frame_ok & (row >= 0) & (row < height), 1.0, 0.0)


def joined(low, high):
    lane = lax.broadcasted_iota(jnp.int32, (low.shape[0], LANES), 1)
    middle = jnp.where(lane < LANES // 2, low[:, LANES:], high[:, :LANES])
    return jnp.concatenate([low[:, :LANES], middle, high[:, LANES:]], axis=-1)


def packed(half, chan):
    return jnp.where(chan == 0, half, pltpu.roll(half, WIDE - C // 2, 1))


def halves(own, other, chan):
    low = jnp.where(chan == 0, own, other)
    high = jnp.where(chan == 0, other, own)
    return joined(low.astype(jnp.float32), high.astype(jnp.float32))


def conv_part(piece, weight, places, col):
    lhs = [piece(place) for place in places]
    cut = slice(col * C, (col + 1) * C)
    rhs = [weight[depth_at * 3 + row_at, :, cut] for depth_at, row_at in places]
    return lax.dot_general(
        jnp.concatenate(lhs, axis=1),
        jnp.concatenate(rhs, axis=1),
        (((1,), (1,)), ((), ())),
        preferred_element_type=jnp.float32,
    )


def columns_summed(parts, span):
    left, here, right = (parts[col, span, :] for col in range(3))
    column = lax.broadcasted_iota(jnp.int32, left.shape, 0)
    left = jnp.where(column == 0, 0.0, pltpu.roll(left, 1, 0))
    right = jnp.where(column == LW - 1, 0.0, pltpu.roll(right, LW - 1, 0))
    return left + here + right


def first_stage(dims, *refs):
    rows_here, height, early, plan = dims
    early_in, early_one, early_two = early
    chunks, refs = list(refs[: len(plan)]), refs[len(plan) :]
    win, other_bias, weight, own_bias_in, gain_in, conv_bias_in, *refs = refs
    second, residual, acts, rows, window, pre, parts, *refs = refs
    own, own_bias, gain, conv_bias, sems = refs
    fetches = []
    for source, target in (
        (chunks[0], own),
        (own_bias_in, own_bias),
        (gain_in, gain),
        (conv_bias_in, conv_bias),
    ):
        fetch = pltpu.make_async_copy(source, target, sems.at[len(fetches)])
        fetch.start()
        fetches.append(fetch)
    space = lax.axis_index("space")
    section = lax.axis_index("tm")
    chan = lax.axis_index("chan")
    row0 = space * rows_here
    groups = LW * ZC // LANES
    lane = lax.broadcasted_iota(jnp.int32, (groups, LANES), 1)
    group = lax.broadcasted_iota(jnp.int32, (groups, LANES), 0)
    low = lane < LANES // 2

    fetches[0].wait()
    chunks[0] = own
    for chunk, (back, turn) in zip(chunks, plan):
        count = chunk.shape[0]
        start = early_in // FS * FS * height - back * FS * height
        if turn is not None:
            blocks = FS * height // count
            start = start + lax.rem(space + (blocks - turn), blocks) * count
        values = chunk[...].astype(jnp.float32)
        for at in range(groups):
            rows[pl.ds(start, count), at, :] = values[:, at * LANES : (at + 1) * LANES]
    for fetch in fetches[1:]:
        fetch.wait()
    mine, other = row_of(own_bias), row_of(other_bias)
    bias = jnp.concatenate(
        [jnp.where(chan == 0, mine, other), jnp.where(chan == 0, other, mine)], axis=1
    )
    lead = early_one - early_two
    frames_one = FS + early_one
    frames_two = FS + early_two

    def run(base, rows_one):
        rows_two = rows_one - 2
        lane_wide = lax.broadcasted_iota(jnp.int32, (rows_one, LW, LANES), 2)

        for frame in range(FS + early_in):
            frame_ok = section * FS - early_in + frame >= 0
            for row in range(rows_one + 2):
                row_abs = row0 - 4 + base + row
                ok = frame_ok & (row_abs >= 0) & (row_abs < height)
                at = frame * height + jnp.clip(row_abs, 0, height - 1)
                here = jnp.where(ok, rows[at], 0.0)
                before = jnp.where(group == 0, 0.0, pltpu.roll(here, 1, 0))
                after = jnp.where(group == groups - 1, 0.0, pltpu.roll(here, groups - 1, 0))
                for col in range(8):
                    source = here
                    if col == 0:
                        source = jnp.where(lane >= LANES - ZC, before, here)
                    if col == 7:
                        source = jnp.where(lane < ZC, after, here)
                    shift = (-ZC * (col - 1)) % LANES
                    one = source if shift == 0 else pltpu.roll(source, shift, 1)
                    two = pltpu.roll(source, (shift + LANES // 2) % LANES, 1)
                    place = window.at[frame, row]
                    place[pl.ds(col, groups, stride=8), :] = jnp.where(low, one, two)

        def input_conv(frame):
            slots = []
            for depth_at in (2, 1, 0):
                source = frame - early_one - 2 + depth_at + early_in
                if source >= 0:
                    slots += [(source, row_at) for row_at in range(3)]
            pieces = []
            for pair in range(0, len(slots), 2):
                source, row_at = slots[pair]
                value = window[source, row_at : row_at + rows_one]
                second_slot = 0.0
                if pair + 1 < len(slots):
                    source, row_at = slots[pair + 1]
                    second_slot = window[source, row_at : row_at + rows_one]
                value = jnp.where(lane_wide < LANES // 2, value, second_slot)
                pieces.append(value.astype(jnp.bfloat16).reshape(rows_one * LW, LANES))
            lhs = jnp.concatenate(pieces, axis=-1)
            pre[frame % 2, 0 : rows_one * LW] = jnp.dot(
                lhs, win[0 : lhs.shape[1]], preferred_element_type=jnp.float32
            )

        def activate(frame, row):
            frame_ok = section * FS - early_one + frame >= 0
            out = pre[frame % 2, row * LW : (row + 1) * LW] + bias
            out = out.astype(jnp.bfloat16).astype(jnp.float32)
            if frame >= early_one:
                mine = jnp.where(
                    chan == 0, out[:, :WIDE], pltpu.roll(out[:, LANES:], C // 2, 1)
                )
                residual[frame - early_one, base + row] = mine.astype(jnp.bfloat16)
            keep = kept(frame_ok, row0 - 3 + base + row, height)
            act = activated(out, row_of(gain) * 0.5, keep)
            acts[frame, base + row] = act.astype(jnp.bfloat16)

        for frame in range(lead + 1):
            input_conv(frame)
            for row in range(rows_one):
                activate(frame, row)
        for frame in range(frames_two - 1):
            later = frame + lead + 1
            row = 0
            input_conv(later)
            for col in range(3):
                first_conv(acts, weight, parts.at[frame % 2], frame, lead, base, rows_two, col)
                while row * 3 < rows_one * (col + 1):
                    activate(later, row)
                    row += 1
            first_finish(parts.at[frame % 2], conv_bias, second.at[frame], base, rows_two)

    by_place(run, rows_here + 6, 2)


def by_place(run, rows, margin):
    count = lax.axis_size("space")
    if count < 2:
        run(0, rows)
        return
    space = lax.axis_index("space")
    outer = (space == 0) | (space == count - 1)

    @pl.when(outer)
    def _():
        run(jnp.where(space == 0, margin, 0), rows - margin)

    @pl.when(jnp.logical_not(outer))
    def _():
        run(0, rows)


def first_conv(acts, weight, parts, frame, lead, base, rows, col):
    places = []
    for depth_at in (2, 1, 0):
        if frame - 2 + depth_at + lead >= 0:
            places += [(depth_at, row_at) for row_at in range(3)]

    def piece(place):
        depth_at, row_at = place
        source = frame - 2 + depth_at + lead
        return acts[source, pl.ds(base + row_at, rows)].reshape(rows * LW, C)

    parts[col, 0 : rows * LW, 0 : C // 2] = conv_part(piece, weight, places, col)


def first_finish(parts, conv_bias, second, base, rows):
    chan = lax.axis_index("chan")
    for row in range(rows):
        total = columns_summed(parts, pl.ds(row * LW, LW))
        total = packed(total + wide_of(conv_bias), chan)
        second[base + row] = total.astype(jnp.bfloat16)
    blank_skipped(second, rows)


def blank_skipped(target, rows):
    skipped = target.shape[0] - rows
    if skipped:
        start = jnp.where(lax.axis_index("space") == 0, 0, rows)
        target[pl.ds(start, skipped)] = jnp.zeros((skipped,) + target.shape[1:], target.dtype)


def first_last(dims, acts, weight, conv_bias, second, parts):
    frame, lead = dims

    def run(base, rows):
        for col in range(3):
            first_conv(acts, weight, parts, frame, lead, base, rows, col)
        first_finish(parts, conv_bias, second, base, rows)

    by_place(run, second.shape[0], 2)


def second_activate(dims, own, other, gain, acts, start, base, rows):
    rows_here, height, early_two = dims
    section = lax.axis_index("tm")
    chan = lax.axis_index("chan")
    row0 = lax.axis_index("space") * rows_here
    half_gain = row_of(gain) * 0.5
    for frame in range(acts.shape[0]):
        frame_ok = section * FS - early_two + start + frame >= 0
        for row in range(rows):
            values = halves(own[frame, base + row], other[frame, base + row], chan)
            keep = kept(frame_ok, row0 - 2 + base + row, height)
            act = activated(values, half_gain, keep)
            acts[frame, base + row] = act.astype(jnp.bfloat16)


def second_lead(dims, own, other, gain, acts):
    def run(base, rows):
        second_activate(dims, own, other, gain, acts, 0, base, rows)

    by_place(run, acts.shape[1], 1)


def second_stage(
    dims, own, other, led, residual, gain, weight, conv_bias, block, acts, parts
):
    early_two = dims[2]
    chan = lax.axis_index("chan")
    ahead = led.shape[0]

    def run(base, rows_two):
        rows = rows_two - 2

        def frame_of(frame, row_at):
            ref, at = (led, frame) if frame < ahead else (acts, frame - ahead)
            return ref[at, pl.ds(base + row_at, rows)].reshape(rows * LW, C)

        def piece(place):
            depth_at, row_at = place
            frames = []
            for frame in range(FS):
                source = frame - 2 + depth_at + early_two
                if source >= 0:
                    frames.append(frame_of(source, row_at))
                else:
                    frames.append(jnp.zeros((rows * LW, C), jnp.bfloat16))
            return jnp.concatenate(frames, axis=0)

        used = (slice(0, FS * rows * LW), slice(0, C // 2))
        taps = [(d, r) for d in (0, 1) for r in range(3) if FS - 3 + d + early_two >= 0]
        for col in range(3):
            if taps:
                parts[(col,) + used] = conv_part(piece, weight, taps, col)
            else:
                parts[col] = jnp.zeros(parts.shape[1:], jnp.float32)
        second_activate(dims, own, other, gain, acts, ahead, base, rows_two)
        for col in range(3):
            taps = [(2, r) for r in range(3)]
            parts[(col,) + used] += conv_part(piece, weight, taps, col)
        for frame in range(FS):
            for row in range(rows):
                total = columns_summed(parts, pl.ds((frame * rows + row) * LW, LW))
                total = total + wide_of(conv_bias)
                total = total + residual[frame, base + row + 2].astype(jnp.float32)
                block[frame, base + row] = packed(total, chan).astype(jnp.bfloat16)
            blank_skipped(block.at[frame], rows)

    by_place(run, led.shape[1], 1)


def third_stage(dims, own, other, weight, up_bias, decoded, acts, raw):
    rows_here, height = dims
    chan = lax.axis_index("chan")
    row0 = lax.axis_index("space") * rows_here
    rows_three = rows_here + 2
    out_chan = weight.shape[1] // 4
    for frame in range(FS):
        for row in range(rows_three):
            values = halves(own[frame, row], other[frame, row], chan)
            values = values * kept(True, row0 - 1 + row, height)
            acts[frame, row] = values.astype(jnp.bfloat16)
    count = FS * rows_here * LW
    source = lax.broadcasted_iota(jnp.int32, (4 * LW, 4 * LW), 0)
    target = lax.broadcasted_iota(jnp.int32, (4 * LW, 4 * LW), 1)
    phase = source // (2 * LW)
    place = source % (2 * LW)
    wanted = (place // LW) * (2 * LW) + (place % LW) * 2 + phase
    shuffle = jnp.where(wanted == target, 1.0, 0.0).astype(jnp.bfloat16)
    column_bias = row_of(up_bias).T
    column = lax.broadcasted_iota(jnp.int32, (out_chan, 2 * LW), 1) % LW
    for row_phase in range(2):
        lhs = [
            acts[:, at : at + rows_here].reshape(count, C)
            for at in (row_phase, row_phase + 1)
        ]
        raw[row_phase] = lax.dot_general(
            weight[row_phase],
            jnp.concatenate(lhs, axis=1),
            (((1,), (1,)), ((), ())),
            preferred_element_type=jnp.float32,
        )
        pairs = []
        for start in range(0, count, 2 * LW):
            left, even, odd, right = (
                raw[row_phase, at * out_chan : (at + 1) * out_chan, start : start + 2 * LW]
                for at in range(4)
            )
            left = jnp.where(column == 0, 0.0, pltpu.roll(left, 1, 1))
            right = jnp.where(column == LW - 1, 0.0, pltpu.roll(right, 2 * LW - 1, 1))
            pair = jnp.concatenate([left + even + column_bias, odd + right + column_bias], axis=1)
            pairs.append(pair.astype(jnp.bfloat16))
        pixels = jnp.dot(
            jnp.concatenate(pairs, axis=0), shuffle, preferred_element_type=jnp.float32
        ).astype(jnp.bfloat16)
        for at in range(len(pairs)):
            frame, row = divmod(2 * at, rows_here)
            part = pixels[at * out_chan : (at + 1) * out_chan]
            decoded[frame, 2 * row + row_phase] = part[:, : 2 * LW]
            decoded[frame, 2 * row + 2 + row_phase] = part[:, 2 * LW :]


def prepare(own_in, other_in, up_in, first_in, win, phases, first, own, up, sems):
    fetches = []
    for source, target in ((own_in, own), (up_in, up), (first_in, first)):
        fetch = pltpu.make_async_copy(source, target, sems.at[len(fetches)])
        fetch.start()
        fetches.append(fetch)
    chan = lax.axis_index("chan")
    fetches[0].wait()
    mine, other = own[...].astype(jnp.float32), other_in[...].astype(jnp.float32)
    low = jnp.where(chan == 0, mine, other)
    high = jnp.where(chan == 0, other, mine)
    joint = jnp.concatenate([low, high], axis=0).T.astype(jnp.bfloat16)
    blank = jnp.zeros((LANES // 2, C), jnp.bfloat16)
    for slot in range(10):
        win[slot * 64 : slot * 64 + 64, :] = blank
    for slot in range(9):
        source = ((2 - slot // 3) * 3 + slot % 3) * 3 * ZC
        win[slot * 64 : slot * 64 + 3 * ZC, :] = joint[source : source + 3 * ZC]
    fetches[1].wait()
    count = up.shape[1]
    for row_phase, split in enumerate((((0,), (1, 2)), ((0, 1), (2,)))):
        for row_at, taps in enumerate(split):
            cols = []
            for c in range(3):
                cut = pl.ds(c * C, C)
                value = up[taps[0], :, cut].astype(jnp.float32)
                for tap in taps[1:]:
                    value = value + up[tap, :, cut].astype(jnp.float32)
                cols.append(value)
            grouped = (cols[0], cols[1] + cols[2], cols[0] + cols[1], cols[2])
            for at, value in enumerate(grouped):
                target = (row_phase, pl.ds(at * count, count), pl.ds(row_at * C, C))
                phases[target] = value.astype(jnp.bfloat16)
    fetches[2].wait()


def limits(mib):
    return pltpu.CompilerParams(vmem_limit_bytes=mib * 1024 * 1024)


def cost(tap_rows):
    return pl.CostEstimate(
        flops=2 * tap_rows * 3 * C * WIDE, bytes_accessed=8 * tap_rows * C, transcendentals=0
    )


def shards(
    latent,
    in_weight,
    in_bias,
    first_gain,
    first_weight,
    first_bias,
    second_gain,
    second_weight,
    second_bias,
    up_weight,
    up_bias,
):
    space_count = lax.axis_size("space")
    tm_count = lax.axis_size("tm")
    rows_here = latent.shape[1] // FS
    height = rows_here * space_count
    groups = LW * ZC // LANES
    earlier = FS * (tm_count - 1)
    early_two, early_one, early_in = min(2, earlier), min(4, earlier), min(6, earlier)
    swap = [(0, 1), (1, 0)]

    plan = []
    if space_count <= 4:
        section_chunks = [latent[0]]
        for turn in range(1, space_count):
            pairs = [(i, (i + turn) % space_count) for i in range(space_count)]
            section_chunks.append(lax.ppermute(latent[0], "space", pairs))
        turns = list(range(space_count))
    else:
        section_chunks = [lax.all_gather(latent[0], "space", axis=0, tiled=True)]
        turns = [None]
    chunks = list(section_chunks)
    plan = [(0, turn) for turn in turns]
    for back in range(1, early_in // FS + 1):
        pairs = [(i, (i + back) % tm_count) for i in range(tm_count)]
        for chunk, turn in zip(section_chunks, turns):
            chunks.append(lax.ppermute(chunk, "tm", pairs))
            plan.append((back, turn))

    stored_in = jnp.swapaxes(in_weight, 0, 1)
    stored_up = jnp.swapaxes(up_weight, 1, 2)
    out_chan = up_weight.shape[-1]
    def stay(array):
        return pltpu.with_memory_space_constraint(array, pltpu.HBM)

    vmem, hbm = pl.BlockSpec(memory_space=pltpu.VMEM), pl.BlockSpec(memory_space=pltpu.HBM)
    stored_first = jnp.swapaxes(first_weight, 1, 2)
    win, phases, fetched_first = pl.pallas_call(
        prepare,
        out_shape=(
            jax.ShapeDtypeStruct((5 * LANES, C), jnp.bfloat16),
            jax.ShapeDtypeStruct((2, 4 * out_chan, 2 * C), jnp.bfloat16),
            jax.ShapeDtypeStruct(stored_first.shape, jnp.bfloat16),
        ),
        in_specs=[hbm, vmem, hbm, hbm],
        out_specs=(vmem,) * 3,
        scratch_shapes=[
            pltpu.VMEM(stored_in.shape, jnp.bfloat16),
            pltpu.VMEM(stored_up.shape, jnp.bfloat16),
            pltpu.SemaphoreType.DMA((3,)),
        ],
        compiler_params=limits(14),
        name="prepare",
    )(
        stay(stored_in),
        lax.ppermute(stored_in, "chan", swap),
        stay(stored_up),
        stay(stored_first),
    )

    rows_two = rows_here + 4
    frames_two = FS + early_two
    ahead = frames_two - 1
    block_shape = (FS, rows_here + 2, LW, WIDE)
    acts_one = (FS + early_one, rows_here + 6, LW, C)
    early = (early_in, early_one, early_two)
    own_lead, residual, acts = pl.pallas_call(
        functools.partial(first_stage, (rows_here, height, early, tuple(plan))),
        out_shape=(
            jax.ShapeDtypeStruct((ahead, rows_two, LW, WIDE), jnp.bfloat16),
            jax.ShapeDtypeStruct((FS, rows_here + 6, LW, WIDE), jnp.bfloat16),
            jax.ShapeDtypeStruct(acts_one, jnp.bfloat16),
        ),
        in_specs=[hbm] + [vmem] * (len(chunks) + 2) + [hbm] * 3,
        out_specs=(vmem,) * 3,
        scratch_shapes=[
            pltpu.VMEM(((FS + early_in) * height, groups, LANES), jnp.float32),
            pltpu.VMEM((FS + early_in, rows_here + 8, LW, LANES), jnp.float32),
            pltpu.VMEM((2, (rows_here + 6) * LW, C), jnp.float32),
            pltpu.VMEM((2, 3, rows_two * LW, WIDE), jnp.float32),
            pltpu.VMEM(chunks[0].shape, jnp.bfloat16),
            pltpu.VMEM(in_bias.shape, jnp.float32),
            pltpu.VMEM(first_gain.shape, jnp.float32),
            pltpu.VMEM(first_bias.shape, jnp.float32),
            pltpu.SemaphoreType.DMA((4,)),
        ],
        compiler_params=limits(20),
        name="first_stage",
    )(
        stay(chunks[0]),
        *chunks[1:],
        win,
        lax.ppermute(in_bias, "chan", swap),
        fetched_first,
        stay(in_bias),
        stay(first_gain),
        stay(first_bias),
    )
    other_lead = lax.ppermute(own_lead, "chan", swap)
    own_last = pl.pallas_call(
        functools.partial(first_last, (ahead, early_one - early_two)),
        out_shape=jax.ShapeDtypeStruct((rows_two, LW, WIDE), jnp.bfloat16),
        in_specs=[vmem] * 3,
        out_specs=vmem,
        scratch_shapes=[pltpu.VMEM((3, rows_two * LW, WIDE), jnp.float32)],
        compiler_params=limits(8),
        name="first_last",
        cost_estimate=cost(9 * rows_two * LW),
    )(acts, fetched_first, first_bias)
    other_last = lax.ppermute(own_last, "chan", swap)

    dims = (rows_here, height, early_two)
    led = pl.pallas_call(
        functools.partial(second_lead, dims),
        out_shape=jax.ShapeDtypeStruct((ahead, rows_two, LW, C), jnp.bfloat16),
        in_specs=[vmem] * 3,
        out_specs=vmem,
        compiler_params=limits(8),
        name="second_lead",
        cost_estimate=cost(2 * rows_two * LW),
    )(own_lead, other_lead, second_gain)
    block_own = pl.pallas_call(
        functools.partial(second_stage, dims),
        out_shape=jax.ShapeDtypeStruct(block_shape, jnp.bfloat16),
        in_specs=[vmem] * 7,
        out_specs=vmem,
        scratch_shapes=[
            pltpu.VMEM((1, rows_two, LW, C), jnp.bfloat16),
            pltpu.VMEM((3, FS * (rows_here + 2) * LW, WIDE), jnp.float32),
        ],
        compiler_params=limits(12),
        name="second_stage",
    )(
        own_last[None],
        other_last[None],
        led,
        residual,
        second_gain,
        jnp.swapaxes(second_weight, 1, 2),
        second_bias,
    )
    block_other = lax.ppermute(block_own, "chan", swap)

    return pl.pallas_call(
        functools.partial(third_stage, (rows_here, height)),
        out_shape=jax.ShapeDtypeStruct((FS, 2 * rows_here, out_chan, 2 * LW), jnp.bfloat16),
        in_specs=[vmem] * 4,
        out_specs=vmem,
        scratch_shapes=[
            pltpu.VMEM((FS, rows_here + 2, LW, C), jnp.bfloat16),
            pltpu.VMEM((2, 4 * out_chan, FS * rows_here * LW), jnp.float32),
        ],
        compiler_params=limits(12),
        name="third_stage",
    )(block_own, block_other, phases, up_bias)


def solution(mesh):
    placed = (
        P(("groups", "tm"), "space", None),
        P(None, "chan"),
        P("chan"),
        P(),
        P(None, None, "chan"),
        P("chan"),
        P(),
        P(None, None, "chan"),
        P("chan"),
        P(None, None, "chan"),
        P("chan"),
    )
    return jax.shard_map(
        shards,
        mesh=mesh,
        in_specs=placed,
        out_specs=P(("groups", "tm"), "space", "chan", None),
        check_vma=False,
    )
```

time: 35.2 us -> 31.9 us (0.906)
  the two profiles are of different devices: /device:TPU:0 before, /device:TPU:13 now
where the time goes in v3:
time: 31.9 us; the launch traced here: 31.7 us
  Pallas kernels  18.2 us (57%)
  starting transfers between devices  11.5 us (36%)
  waiting for transfers between devices  1.88 us (6%)
    pallas_call x1, Pallas kernels, shards(): pl.pallas_call(functools.partial(first_stage, (rows_here, height, early,...  7.47 us
    ppermute x3, starting transfers between devices, shards(): section_chunks.append(lax.ppermute(latent[0], 'space', pairs))  4.67 us
    pallas_call x1, Pallas kernels, shards(): pl.pallas_call(functools.partial(second_stage, dims), out_shape=jax.Shape...  3.22 us
    ppermute x4, starting transfers between devices, shards(): chunks.append(lax.ppermute(chunk, 'tm', pairs))  2.93 us
    pallas_call x1, Pallas kernels, shards(): pl.pallas_call(prepare, out_shape=(jax.ShapeDtypeStruct((5 * LANES, C), j...  2.48 us
    pallas_call x1, Pallas kernels, shards(): pl.pallas_call(functools.partial(first_last, (ahead, early_one - early_tw...  2.44 us
    ppermute x1, starting transfers between devices, shards(): lax.ppermute(in_bias, 'chan', swap)  1.96 us
    pallas_call x1, Pallas kernels, shards(): pl.pallas_call(functools.partial(third_stage, (rows_here, height)), out_s...  1.94 us
  transfers between devices with their start and end apart: 12, of which 2 were waited for; matrix products, arithmetic and copies ran while one was open for 0% of the time, Pallas kernels for 18%

profile of v3, /device:TPU:13, one launch (start us, length us, event | category | flops | bytes accessed | tf_op | source)
XLA Modules:
  0.0 31.7 jit_solution(17673357846548469573)
XLA Ops:
  0.0 0.7 %collective-permute-start.7 = (bf16[192,432]{1,0:T(8,128)(2,1)}, bf16[192,432]{1,0:T(8,128)(2,1)S(1)}, u32[]{:S(2)}, u32[]{:S(2)}) collective-permute-start(bf16[192,432]{1,0:T(8,128)(2,1)} %bitcast.12), channel_id=1, source_target_pairs={{0,1},{1,0},{2,3},{3,2},{4,5},{5,4},{6,7},{7,6},{8,9},{9,8},{10,11... | collective-permute-start | bytes 497672 | tf_op jit(solution)/shard_map/ppermute | solution.py:490
  0.7 0.2 collective-permute-start.2
  0.8 2.3 %collective-permute-start.1 = (bf16[4,1024]{1,0:T(4,128)(2,1)}, bf16[4,1024]{1,0:T(4,128)(2,1)S(1)}, u32[]{:S(2)}, u32[]{:S(2)}) collective-permute-start(bf16[4,1024]{1,0:T(4,128)(2,1)} %bitcast.15), channel_id=1, source_target_pairs={{0,8},{4,12},{8,0},{12,4},{1,9},{5,13},{9,1},{13,5},{2,10},{6,14},... | collective-permute-start | bytes 24584 | tf_op jit(solution)/shard_map/ppermute | solution.py:451
  3.2 2.2 %collective-permute-start = (bf16[4,1024]{1,0:T(4,128)(2,1)}, bf16[4,1024]{1,0:T(4,128)(2,1)S(1)}, u32[]{:S(2)}, u32[]{:S(2)}) collective-permute-start(bf16[4,1024]{1,0:T(4,128)(2,1)} %bitcast.16), channel_id=1, source_target_pairs={{0,4},{4,8},{8,12},{12,0},{1,5},{5,9},{9,13},{13,1},{2,6},{6,10},{... | collective-permute-start | bytes 24584 | tf_op jit(solution)/shard_map/ppermute | solution.py:451
  5.4 1.2 %collective-permute-start.3 = (bf16[4,1024]{1,0:T(4,128)(2,1)}, bf16[4,1024]{1,0:T(4,128)(2,1)S(1)}, u32[]{:S(2)}, u32[]{:S(2)}) collective-permute-start(bf16[4,1024]{1,0:T(4,128)(2,1)} %bitcast.17), channel_id=1, source_target_pairs={{0,2},{2,0},{1,3},{3,1},{4,6},{6,4},{5,7},{7,5},{8,10},{10,8},{9,1... | collective-permute-start | bytes 24584 | tf_op jit(solution)/shard_map/ppermute | solution.py:461
  6.6 0.0 collective-permute-done.2.refs_3_
  6.6 0.3 collective-permute-start.6
  6.8 1.2 %collective-permute-start.5 = (bf16[4,1024]{1,0:T(4,128)(2,1)S(1)}, bf16[4,1024]{1,0:T(4,128)(2,1)S(1)}, u32[]{:S(2)}, u32[]{:S(2)}) collective-permute-start(bf16[4,1024]{1,0:T(4,128)(2,1)S(1)} %collective-permute-done.1.refs_2_), channel_id=1, source_target_pairs={{0,2},{2,0},{1,3},{3,1},{4,6},{6,4},{5,7},{7,5},{8,10},{10,8},{9,1... | collective-permute-start | bytes 24584 | tf_op jit(solution)/shard_map/ppermute | solution.py:461
  8.0 0.3 collective-permute-start.4
  8.3 0.0 collective-permute-done.7.other_in
  8.3 2.0 %collective-permute-start.8 = (f32[192]{0:T(256)}, f32[192]{0:T(256)S(1)}, u32[]{:S(2)}, u32[]{:S(2)}) collective-permute-start(f32[192]{0:T(256)} %refs_11_.1), channel_id=1, source_target_pairs={{0,1},{1,0},{2,3},{3,2},{4,5},{5,4},{6,7},{7,6},{8,9},{9,8},{10,11... | collective-permute-start | bytes 2312 | tf_op jit(solution)/shard_map/ppermute | solution.py:527
  10.3 2.5 %prepare.1 = (bf16[640,384]{1,0:T(8,128)(2,1)S(1)}, bf16[2,384,768]{2,1,0:T(8,128)(2,1)S(1)}, bf16[9,192,1152]{2,1,0:T(8,128)(2,1)S(1)}) custom-call(bf16[192,432]{1,0:T(8,128)(2,1)} %bitcast.13, bf16[192,432]{1,0:T(8,128)(2,1)S(1)} %collective-permute-done.7.other_in, bf16[3,96,1152]{2,1,0:T(8,128)(2,1)} %bitcast.11, bf16[9,192,1152]{2,1,0:T(8,128)(2,1)} %bitcast.10), custom_call_target="tpu_custom_call" | custom-call | tf_op jit(solution)/shard_map/prepare/pallas_call | solution.py:472
  12.8 7.5 %first_stage.1 = (bf16[3,6,64,256]{3,2,1,0:T(8,128)(2,1)S(1)}, bf16[2,8,64,256]{3,2,1,0:T(8,128)(2,1)S(1)}, bf16[4,8,64,384]{3,2,1,0:T(8,128)(2,1)S(1)}) custom-call(bf16[4,1024]{1,0:T(4,128)(2,1)} %bitcast.18, bf16[4,1024]{1,0:T(4,128)(2,1)S(1)} %collective-permute-done.refs_1_, bf16[4,1024]{1,0:T(4,128)(2,1)S(1)} %collective-permute-done.1.refs_2_, ...), custom_call_target="tpu_custom_call" | custom-call | tf_op jit(solution)/shard_map/first_stage/pallas_call | solution.py:501
  20.3 0.0 copy-start.1
  20.3 0.6 %collective-permute-start.10 = (bf16[3,6,64,256]{3,2,1,0:T(8,128)(2,1)S(1)}, bf16[3,6,64,256]{3,2,1,0:T(8,128)(2,1)S(1)}, u32[]{:S(2)}, u32[]{:S(2)}) collective-permute-start(bf16[3,6,64,256]{3,2,1,0:T(8,128)(2,1)S(1)} %get-tuple-element.14.own), channel_id=1, source_target_pairs={{0,1},{1,0},{2,3},{3,2},{4,5},{5,4},{6,7},{7,6},{8,9},{9,8},{10,11... | collective-permute-start | bytes 1769480 | tf_op jit(solution)/shard_map/ppermute | solution.py:533
  20.9 2.4 %first_last.1 = bf16[6,64,256]{2,1,0:T(8,128)(2,1)S(1)} custom-call(bf16[4,8,64,384]{3,2,1,0:T(8,128)(2,1)S(1)} %get-tuple-element.13.acts, bf16[9,192,1152]{2,1,0:T(8,128)(2,1)S(1)} %get-tuple-element.12.refs_10_.weight, f32[192]{0:T(256)S(1)} %copy-done.2), custom_call_target="tpu_custom_call" | custom-call | flops 2038431744 | bytes 10616832 | tf_op jit(solution)/shard_map/first_last/pallas_call | solution.py:534
  23.4 0.0 copy-start.4
  23.4 0.3 collective-permute-start.9
  23.7 0.6 %second_lead.1.led = bf16[3,6,64,384]{3,2,1,0:T(8,128)(2,1)S(1)} custom-call(bf16[3,6,64,256]{3,2,1,0:T(8,128)(2,1)S(1)} %get-tuple-element.14.own, bf16[3,6,64,256]{3,2,1,0:T(8,128)(2,1)S(1)} %collective-permute-done.10.other, f32[384]{0:T(512)S(1)} %copy-done.1), custom_call_target="tpu_custom_call" | custom-call | flops 452984832 | bytes 2359296 | tf_op jit(solution)/shard_map/second_lead/pallas_call | solution.py:547
  24.4 0.6 %collective-permute-done.9 = bf16[6,64,256]{2,1,0:T(8,128)(2,1)S(1)} collective-permute-done((bf16[6,64,256]{2,1,0:T(8,128)(2,1)S(1)}, bf16[6,64,256]{2,1,0:T(8,128)(2,1)S(1)}, u32[]{:S(2)}, u32[]{:S(2)}) %collective-permute-start.9) | collective-permute-done | bytes 196640 | tf_op jit(solution)/shard_map/ppermute | solution.py:544
  24.9 3.2 %second_stage.1.own = bf16[2,4,64,256]{3,2,1,0:T(8,128)(2,1)S(1)} custom-call(bf16[1,6,64,256]{3,2,1,0:T(8,128)(2,1)S(1)} %bitcast.8, bf16[1,6,64,256]{3,2,1,0:T(8,128)(2,1)S(1)} %bitcast.9, bf16[3,6,64,384]{3,2,1,0:T(8,128)(2,1)S(1)} %second_lead.1.led, bf16[2,8,64,256]{3,2,1,0:T(8,128)(2,1)S(1)} %get-tuple-element.15.residual, f32[384]{0:T(512)S(1)} %copy-done.1, ...), custom_call_target="tpu_custom_call" | custom-call | tf_op jit(solution)/shard_map/second_stage/pallas_call | solution.py:556
  28.1 0.3 collective-permute-start.11
  28.4 1.3 %collective-permute-done.11.other = bf16[2,4,64,256]{3,2,1,0:T(8,128)(2,1)S(1)} collective-permute-done((bf16[2,4,64,256]{3,2,1,0:T(8,128)(2,1)S(1)}, bf16[2,4,64,256]{3,2,1,0:T(8,128)(2,1)S(1)}, u32[]{:S(2)}, u32[]{:S(2)}) %collective-permute-start.11) | collective-permute-done | bytes 262176 | tf_op jit(solution)/shard_map/ppermute | solution.py:576
  29.7 1.9 %third_stage.1 = bf16[2,4,96,128]{3,2,1,0:T(8,128)(2,1)} custom-call(bf16[2,4,64,256]{3,2,1,0:T(8,128)(2,1)S(1)} %second_stage.1.own, bf16[2,4,64,256]{3,2,1,0:T(8,128)(2,1)S(1)} %collective-permute-done.11.other, bf16[2,384,768]{2,1,0:T(8,128)(2,1)S(1)} %get-tuple-element.16.weight, f32[96]{0:T(128)S(1)} %copy-done.4), custom_call_target="tpu_custom_call" | custom-call | tf_op jit(solution)/shard_map/third_stage/pallas_call | solution.py:578
  (16 shorter events, 0.0 us)
Async XLA Ops:
  0.0 8.3 %collective-permute-start.7 = (bf16[192,432]{1,0:T(8,128)(2,1)}, bf16[192,432]{1,0:T(8,128)(2,1)S(1)}, u32[]{:S(2)}, u32[]{:S(2)}) collective-permute-start(bf16[192,432]{1,0:T(8,128)(2,1)} %bitcast.12), channel_id=1, source_target_pairs={{0,1},{1,0},{2,3},{3,2},{4,5},{5,4},{6,7},{7,6},{8,9},{9,8},{10,11... | collective-permute-start | bytes 497672 | tf_op jit(solution)/shard_map/ppermute | solution.py:490
  0.7 5.9 %collective-permute-start.2 = (bf16[4,1024]{1,0:T(4,128)(2,1)}, bf16[4,1024]{1,0:T(4,128)(2,1)S(1)}, u32[]{:S(2)}, u32[]{:S(2)}) collective-permute-start(bf16[4,1024]{1,0:T(4,128)(2,1)} %bitcast.14), channel_id=1, source_target_pairs={{0,12},{4,0},{8,4},{12,8},{1,13},{5,1},{9,5},{13,9},{2,14},{6,2},{... | collective-permute-start | bytes 24584 | tf_op jit(solution)/shard_map/ppermute | solution.py:451
  0.8 6.0 %collective-permute-start.1 = (bf16[4,1024]{1,0:T(4,128)(2,1)}, bf16[4,1024]{1,0:T(4,128)(2,1)S(1)}, u32[]{:S(2)}, u32[]{:S(2)}) collective-permute-start(bf16[4,1024]{1,0:T(4,128)(2,1)} %bitcast.15), channel_id=1, source_target_pairs={{0,8},{4,12},{8,0},{12,4},{1,9},{5,13},{9,1},{13,5},{2,10},{6,14},... | collective-permute-start | bytes 24584 | tf_op jit(solution)/shard_map/ppermute | solution.py:451
  3.2 4.9 %collective-permute-start = (bf16[4,1024]{1,0:T(4,128)(2,1)}, bf16[4,1024]{1,0:T(4,128)(2,1)S(1)}, u32[]{:S(2)}, u32[]{:S(2)}) collective-permute-start(bf16[4,1024]{1,0:T(4,128)(2,1)} %bitcast.16), channel_id=1, source_target_pairs={{0,4},{4,8},{8,12},{12,0},{1,5},{5,9},{9,13},{13,1},{2,6},{6,10},{... | collective-permute-start | bytes 24584 | tf_op jit(solution)/shard_map/ppermute | solution.py:451
  5.4 7.4 %collective-permute-start.3 = (bf16[4,1024]{1,0:T(4,128)(2,1)}, bf16[4,1024]{1,0:T(4,128)(2,1)S(1)}, u32[]{:S(2)}, u32[]{:S(2)}) collective-permute-start(bf16[4,1024]{1,0:T(4,128)(2,1)} %bitcast.17), channel_id=1, source_target_pairs={{0,2},{2,0},{1,3},{3,1},{4,6},{6,4},{5,7},{7,5},{8,10},{10,8},{9,1... | collective-permute-start | bytes 24584 | tf_op jit(solution)/shard_map/ppermute | solution.py:461
  6.6 6.2 %collective-permute-start.6 = (bf16[4,1024]{1,0:T(4,128)(2,1)S(1)}, bf16[4,1024]{1,0:T(4,128)(2,1)S(1)}, u32[]{:S(2)}, u32[]{:S(2)}) collective-permute-start(bf16[4,1024]{1,0:T(4,128)(2,1)S(1)} %collective-permute-done.2.refs_3_), channel_id=1, source_target_pairs={{0,2},{2,0},{1,3},{3,1},{4,6},{6,4},{5,7},{7,5},{8,10},{10,8},{9,1... | collective-permute-start | bytes 24584 | tf_op jit(solution)/shard_map/ppermute | solution.py:461
  6.8 6.0 %collective-permute-start.5 = (bf16[4,1024]{1,0:T(4,128)(2,1)S(1)}, bf16[4,1024]{1,0:T(4,128)(2,1)S(1)}, u32[]{:S(2)}, u32[]{:S(2)}) collective-permute-start(bf16[4,1024]{1,0:T(4,128)(2,1)S(1)} %collective-permute-done.1.refs_2_), channel_id=1, source_target_pairs={{0,2},{2,0},{1,3},{3,1},{4,6},{6,4},{5,7},{7,5},{8,10},{10,8},{9,1... | collective-permute-start | bytes 24584 | tf_op jit(solution)/shard_map/ppermute | solution.py:461
  8.0 4.8 %collective-permute-start.4 = (bf16[4,1024]{1,0:T(4,128)(2,1)S(1)}, bf16[4,1024]{1,0:T(4,128)(2,1)S(1)}, u32[]{:S(2)}, u32[]{:S(2)}) collective-permute-start(bf16[4,1024]{1,0:T(4,128)(2,1)S(1)} %collective-permute-done.refs_1_), channel_id=1, source_target_pairs={{0,2},{2,0},{1,3},{3,1},{4,6},{6,4},{5,7},{7,5},{8,10},{10,8},{9,1... | collective-permute-start | bytes 24584 | tf_op jit(solution)/shard_map/ppermute | solution.py:461
  8.3 4.5 %collective-permute-start.8 = (f32[192]{0:T(256)}, f32[192]{0:T(256)S(1)}, u32[]{:S(2)}, u32[]{:S(2)}) collective-permute-start(f32[192]{0:T(256)} %refs_11_.1), channel_id=1, source_target_pairs={{0,1},{1,0},{2,3},{3,2},{4,5},{5,4},{6,7},{7,6},{8,9},{9,8},{10,11... | collective-permute-start | bytes 2312 | tf_op jit(solution)/shard_map/ppermute | solution.py:527
  10.3 10.7 %copy-start.2 = (f32[192]{0:T(256)S(1)}, f32[192]{0:T(256)}, u32[]{:S(2)}) copy-start(f32[192]{0:T(256)} %conv_bias.2) | copy-start | bytes 2308
  20.3 3.4 %copy-start.1 = (f32[384]{0:T(512)S(1)}, f32[384]{0:T(512)}, u32[]{:S(2)}) copy-start(f32[384]{0:T(512)} %gain.3) | copy-start | bytes 4612
  20.3 3.4 %collective-permute-start.10 = (bf16[3,6,64,256]{3,2,1,0:T(8,128)(2,1)S(1)}, bf16[3,6,64,256]{3,2,1,0:T(8,128)(2,1)S(1)}, u32[]{:S(2)}, u32[]{:S(2)}) collective-permute-start(bf16[3,6,64,256]{3,2,1,0:T(8,128)(2,1)S(1)} %get-tuple-element.14.own), channel_id=1, source_target_pairs={{0,1},{1,0},{2,3},{3,2},{4,5},{5,4},{6,7},{7,6},{8,9},{9,8},{10,11... | collective-permute-start | bytes 1769480 | tf_op jit(solution)/shard_map/ppermute | solution.py:533
  20.9 4.0 %copy-start = (bf16[9,1152,192]{1,2,0:T(8,128)(2,1)S(1)}, bf16[9,1152,192]{1,2,0:T(8,128)(2,1)}, u32[]{:S(2)}) copy-start(bf16[9,1152,192]{1,2,0:T(8,128)(2,1)} %param.18) | copy-start | bytes 11943940
  20.9 4.0 %copy-start.3 = (f32[192]{0:T(256)S(1)}, f32[192]{0:T(256)}, u32[]{:S(2)}) copy-start(f32[192]{0:T(256)} %conv_bias.3) | copy-start | bytes 2308
  23.4 6.4 %copy-start.4 = (f32[96]{0:T(128)S(1)}, f32[96]{0:T(128)}, u32[]{:S(2)}) copy-start(f32[96]{0:T(128)} %up_bias.1) | copy-start | bytes 1156
  23.4 1.5 %collective-permute-start.9 = (bf16[6,64,256]{2,1,0:T(8,128)(2,1)S(1)}, bf16[6,64,256]{2,1,0:T(8,128)(2,1)S(1)}, u32[]{:S(2)}, u32[]{:S(2)}) collective-permute-start(bf16[6,64,256]{2,1,0:T(8,128)(2,1)S(1)} %first_last.1), channel_id=1, source_target_pairs={{0,1},{1,0},{2,3},{3,2},{4,5},{5,4},{6,7},{7,6},{8,9},{9,8},{10,11... | collective-permute-start | bytes 589832 | tf_op jit(solution)/shard_map/ppermute | solution.py:544
  28.1 1.6 %collective-permute-start.11 = (bf16[2,4,64,256]{3,2,1,0:T(8,128)(2,1)S(1)}, bf16[2,4,64,256]{3,2,1,0:T(8,128)(2,1)S(1)}, u32[]{:S(2)}, u32[]{:S(2)}) collective-permute-start(bf16[2,4,64,256]{3,2,1,0:T(8,128)(2,1)S(1)} %second_stage.1.own), channel_id=1, source_target_pairs={{0,1},{1,0},{2,3},{3,2},{4,5},{5,4},{6,7},{7,6},{8,9},{9,8},{10,11... | collective-permute-start | bytes 786440 | tf_op jit(solution)/shard_map/ppermute | solution.py:576

commit v4 on v3

--- a/solution.py
+++ b/solution.py
@@ -67,9 +67,11 @@
 
 def columns_summed(parts, span):
     left, here, right = (parts[col, span, :] for col in range(3))
-    column = lax.broadcasted_iota(jnp.int32, left.shape, 0)
-    left = jnp.where(column == 0, 0.0, pltpu.roll(left, 1, 0))
-    right = jnp.where(column == LW - 1, 0.0, pltpu.roll(right, LW - 1, 0))
+    group = lax.broadcasted_iota(jnp.int32, (8, WIDE), 0)
+    wrapped = jnp.where(group == 0, 0.0, pltpu.roll(left[LW - 8 :], 1, 0))
+    left = jnp.concatenate([wrapped, left[: LW - 8]], axis=0)
+    wrapped = jnp.where(group == 7, 0.0, pltpu.roll(right[:8], 7, 0))
+    right = jnp.concatenate([right[8:], wrapped], axis=0)
     return left + here + right
 
 
@@ -142,8 +144,7 @@
                     shift = (-ZC * (col - 1)) % LANES
                     one = source if shift == 0 else pltpu.roll(source, shift, 1)
                     two = pltpu.roll(source, (shift + LANES // 2) % LANES, 1)
-                    place = window.at[frame, row]
-                    place[pl.ds(col, groups, stride=8), :] = jnp.where(low, one, two)
+                    window[frame, row, col * 8 : col * 8 + 8, :] = jnp.where(low, one, two)
 
         def input_conv(frame):
             slots = []
@@ -340,10 +341,11 @@
     target = lax.broadcasted_iota(jnp.int32, (4 * LW, 4 * LW), 1)
     phase = source // (2 * LW)
     place = source % (2 * LW)
-    wanted = (place // LW) * (2 * LW) + (place % LW) * 2 + phase
+    column = place % 8 * 8 + place % LW // 8
+    wanted = (place // LW) * (2 * LW) + column * 2 + phase
     shuffle = jnp.where(wanted == target, 1.0, 0.0).astype(jnp.bfloat16)
     column_bias = row_of(up_bias).T
-    column = lax.broadcasted_iota(jnp.int32, (out_chan, 2 * LW), 1) % LW
+    place = lax.broadcasted_iota(jnp.int32, (out_chan, 2 * LW), 1) % LW
     for row_phase in range(2):
         lhs = [
             acts[:, at : at + rows_here].reshape(count, C)
@@ -355,24 +357,28 @@
             (((1,), (1,)), ((), ())),
             preferred_element_type=jnp.float32,
         )
-        pairs = []
+    pairs, targets = [], []
+    for row_phase in range(2):
         for start in range(0, count, 2 * LW):
             left, even, odd, right = (
                 raw[row_phase, at * out_chan : (at + 1) * out_chan, start : start + 2 * LW]
                 for at in range(4)
             )
-            left = jnp.where(column == 0, 0.0, pltpu.roll(left, 1, 1))
-            right = jnp.where(column == LW - 1, 0.0, pltpu.roll(right, 2 * LW - 1, 1))
+            wrapped = jnp.where(place == 0, 0.0, pltpu.roll(left, 2 * LW - (LW - 9), 1))
+            left = jnp.where(place < 8, wrapped, pltpu.roll(left, 8, 1))
+            wrapped = jnp.where(place == LW - 1, 0.0, pltpu.roll(right, LW - 9, 1))
+            right = jnp.where(place >= LW - 8, wrapped, pltpu.roll(right, 2 * LW - 8, 1))
             pair = jnp.concatenate([left + even + column_bias, odd + right + column_bias], axis=1)
             pairs.append(pair.astype(jnp.bfloat16))
-        pixels = jnp.dot(
-            jnp.concatenate(pairs, axis=0), shuffle, preferred_element_type=jnp.float32
-        ).astype(jnp.bfloat16)
-        for at in range(len(pairs)):
-            frame, row = divmod(2 * at, rows_here)
-            part = pixels[at * out_chan : (at + 1) * out_chan]
-            decoded[frame, 2 * row + row_phase] = part[:, : 2 * LW]
-            decoded[frame, 2 * row + 2 + row_phase] = part[:, 2 * LW :]
+            frame, row = divmod(start // LW, rows_here)
+            targets.append((frame, 2 * row + row_phase))
+    pixels = jnp.dot(
+        jnp.concatenate(pairs, axis=0), shuffle, preferred_element_type=jnp.float32
+    ).astype(jnp.bfloat16)
+    for at, (frame, row) in enumerate(targets):
+        part = pixels[at * out_chan : (at + 1) * out_chan]
+        decoded[frame, row] = part[:, : 2 * LW]
+        decoded[frame, row + 2] = part[:, 2 * LW :]
 
 
 def prepare(own_in, other_in, up_in, first_in, win, phases, first, own, up, sems):
@@ -464,6 +470,7 @@
     stored_in = jnp.swapaxes(in_weight, 0, 1)
     stored_up = jnp.swapaxes(up_weight, 1, 2)
     out_chan = up_weight.shape[-1]
+    other_bias = lax.ppermute(in_bias, "chan", swap)
     def stay(array):
         return pltpu.with_memory_space_constraint(array, pltpu.HBM)
 
@@ -524,7 +531,7 @@
         stay(chunks[0]),
         *chunks[1:],
         win,
-        lax.ppermute(in_bias, "chan", swap),
+        other_bias,
         fetched_first,
         stay(in_bias),
         stay(first_gain),

time: 31.9 us -> 31.4 us (0.984)
  Pallas kernels: 18.2 us -> 17.7 us
    pallas_call x1, Pallas kernels: 1.94 us -> 1.53 us  [shards(): pl.pallas_call(functools.partial(third_stage, (rows_here, height)), out_s...]
where the time goes in v4:
time: 31.4 us; the launch traced here: 31.2 us
  Pallas kernels  17.7 us (56%)
  starting transfers between devices  11.5 us (37%)
  waiting for transfers between devices  1.87 us (6%)
    pallas_call x1, Pallas kernels, shards(): pl.pallas_call(functools.partial(first_stage, (rows_here, height, early,...  7.41 us
    ppermute x3, starting transfers between devices, shards(): section_chunks.append(lax.ppermute(latent[0], 'space', pairs))  4.67 us
    pallas_call x1, Pallas kernels, shards(): pl.pallas_call(functools.partial(second_stage, dims), out_shape=jax.Shape...  3.21 us
    ppermute x4, starting transfers between devices, shards(): chunks.append(lax.ppermute(chunk, 'tm', pairs))  2.93 us
    pallas_call x1, Pallas kernels, shards(): pl.pallas_call(prepare, out_shape=(jax.ShapeDtypeStruct((5 * LANES, C), j...  2.48 us
    pallas_call x1, Pallas kernels, shards(): pl.pallas_call(functools.partial(first_last, (ahead, early_one - early_tw...  2.43 us
    ppermute x1, starting transfers between devices, shards(): other_bias = lax.ppermute(in_bias, 'chan', swap)  1.96 us
    pallas_call x1, Pallas kernels, shards(): pl.pallas_call(functools.partial(third_stage, (rows_here, height)), out_s...  1.53 us
  transfers between devices with their start and end apart: 12, of which 2 were waited for; matrix products, arithmetic and copies ran while one was open for 0% of the time, Pallas kernels for 18%

profile of v4, /device:TPU:13, one launch (start us, length us, event | category | flops | bytes accessed | tf_op | source)
XLA Modules:
  0.0 31.2 jit_solution(8202274877449390344)
XLA Ops:
  0.0 0.7 %collective-permute-start.7 = (bf16[192,432]{1,0:T(8,128)(2,1)}, bf16[192,432]{1,0:T(8,128)(2,1)S(1)}, u32[]{:S(2)}, u32[]{:S(2)}) collective-permute-start(bf16[192,432]{1,0:T(8,128)(2,1)} %bitcast.12), channel_id=1, source_target_pairs={{0,1},{1,0},{2,3},{3,2},{4,5},{5,4},{6,7},{7,6},{8,9},{9,8},{10,11... | collective-permute-start | bytes 497672 | tf_op jit(solution)/shard_map/ppermute | solution.py:497
  0.7 0.2 collective-permute-start.2
  0.8 2.3 %collective-permute-start.1 = (bf16[4,1024]{1,0:T(4,128)(2,1)}, bf16[4,1024]{1,0:T(4,128)(2,1)S(1)}, u32[]{:S(2)}, u32[]{:S(2)}) collective-permute-start(bf16[4,1024]{1,0:T(4,128)(2,1)} %bitcast.15), channel_id=1, source_target_pairs={{0,8},{4,12},{8,0},{12,4},{1,9},{5,13},{9,1},{13,5},{2,10},{6,14},... | collective-permute-start | bytes 24584 | tf_op jit(solution)/shard_map/ppermute | solution.py:457
  3.2 2.2 %collective-permute-start = (bf16[4,1024]{1,0:T(4,128)(2,1)}, bf16[4,1024]{1,0:T(4,128)(2,1)S(1)}, u32[]{:S(2)}, u32[]{:S(2)}) collective-permute-start(bf16[4,1024]{1,0:T(4,128)(2,1)} %bitcast.16), channel_id=1, source_target_pairs={{0,4},{4,8},{8,12},{12,0},{1,5},{5,9},{9,13},{13,1},{2,6},{6,10},{... | collective-permute-start | bytes 24584 | tf_op jit(solution)/shard_map/ppermute | solution.py:457
  5.4 1.2 %collective-permute-start.3 = (bf16[4,1024]{1,0:T(4,128)(2,1)}, bf16[4,1024]{1,0:T(4,128)(2,1)S(1)}, u32[]{:S(2)}, u32[]{:S(2)}) collective-permute-start(bf16[4,1024]{1,0:T(4,128)(2,1)} %bitcast.17), channel_id=1, source_target_pairs={{0,2},{2,0},{1,3},{3,1},{4,6},{6,4},{5,7},{7,5},{8,10},{10,8},{9,1... | collective-permute-start | bytes 24584 | tf_op jit(solution)/shard_map/ppermute | solution.py:467
  6.6 0.0 collective-permute-done.2.refs_3_
  6.6 0.3 collective-permute-start.6
  6.8 0.0 collective-permute-done.1.refs_2_
  6.8 1.2 %collective-permute-start.5 = (bf16[4,1024]{1,0:T(4,128)(2,1)S(1)}, bf16[4,1024]{1,0:T(4,128)(2,1)S(1)}, u32[]{:S(2)}, u32[]{:S(2)}) collective-permute-start(bf16[4,1024]{1,0:T(4,128)(2,1)S(1)} %collective-permute-done.1.refs_2_), channel_id=1, source_target_pairs={{0,2},{2,0},{1,3},{3,1},{4,6},{6,4},{5,7},{7,5},{8,10},{10,8},{9,1... | collective-permute-start | bytes 24584 | tf_op jit(solution)/shard_map/ppermute | solution.py:467
  8.0 0.3 collective-permute-start.4
  8.3 2.0 %collective-permute-start.8 = (f32[192]{0:T(256)}, f32[192]{0:T(256)S(1)}, u32[]{:S(2)}, u32[]{:S(2)}) collective-permute-start(f32[192]{0:T(256)} %refs_11_.1), channel_id=1, source_target_pairs={{0,1},{1,0},{2,3},{3,2},{4,5},{5,4},{6,7},{7,6},{8,9},{9,8},{10,11... | collective-permute-start | bytes 2312 | tf_op jit(solution)/shard_map/ppermute | solution.py:473
  10.3 2.5 %prepare.1 = (bf16[640,384]{1,0:T(8,128)(2,1)S(1)}, bf16[2,384,768]{2,1,0:T(8,128)(2,1)S(1)}, bf16[9,192,1152]{2,1,0:T(8,128)(2,1)S(1)}) custom-call(bf16[192,432]{1,0:T(8,128)(2,1)} %bitcast.13, bf16[192,432]{1,0:T(8,128)(2,1)S(1)} %collective-permute-done.7.other_in, bf16[3,96,1152]{2,1,0:T(8,128)(2,1)} %bitcast.11, bf16[9,192,1152]{2,1,0:T(8,128)(2,1)} %bitcast.10), custom_call_target="tpu_custom_call" | custom-call | tf_op jit(solution)/shard_map/prepare/pallas_call | solution.py:479
  12.8 7.4 %first_stage.1 = (bf16[3,6,64,256]{3,2,1,0:T(8,128)(2,1)S(1)}, bf16[2,8,64,256]{3,2,1,0:T(8,128)(2,1)S(1)}, bf16[4,8,64,384]{3,2,1,0:T(8,128)(2,1)S(1)}) custom-call(bf16[4,1024]{1,0:T(4,128)(2,1)} %bitcast.18, bf16[4,1024]{1,0:T(4,128)(2,1)S(1)} %collective-permute-done.refs_1_, bf16[4,1024]{1,0:T(4,128)(2,1)S(1)} %collective-permute-done.1.refs_2_, ...), custom_call_target="tpu_custom_call" | custom-call | tf_op jit(solution)/shard_map/first_stage/pallas_call | solution.py:508
  20.2 0.0 copy-start.1
  20.2 0.6 %collective-permute-start.10 = (bf16[3,6,64,256]{3,2,1,0:T(8,128)(2,1)S(1)}, bf16[3,6,64,256]{3,2,1,0:T(8,128)(2,1)S(1)}, u32[]{:S(2)}, u32[]{:S(2)}) collective-permute-start(bf16[3,6,64,256]{3,2,1,0:T(8,128)(2,1)S(1)} %get-tuple-element.14.own), channel_id=1, source_target_pairs={{0,1},{1,0},{2,3},{3,2},{4,5},{5,4},{6,7},{7,6},{8,9},{9,8},{10,11... | collective-permute-start | bytes 1769480 | tf_op jit(solution)/shard_map/ppermute | solution.py:540
  20.9 2.4 %first_last.1 = bf16[6,64,256]{2,1,0:T(8,128)(2,1)S(1)} custom-call(bf16[4,8,64,384]{3,2,1,0:T(8,128)(2,1)S(1)} %get-tuple-element.13.acts, bf16[9,192,1152]{2,1,0:T(8,128)(2,1)S(1)} %get-tuple-element.12.refs_10_.weight, f32[192]{0:T(256)S(1)} %copy-done.2), custom_call_target="tpu_custom_call" | custom-call | flops 2038431744 | bytes 10616832 | tf_op jit(solution)/shard_map/first_last/pallas_call | solution.py:541
  23.3 0.0 copy-start.4
  23.3 0.3 collective-permute-start.9
  23.6 0.6 %second_lead.1.led = bf16[3,6,64,384]{3,2,1,0:T(8,128)(2,1)S(1)} custom-call(bf16[3,6,64,256]{3,2,1,0:T(8,128)(2,1)S(1)} %get-tuple-element.14.own, bf16[3,6,64,256]{3,2,1,0:T(8,128)(2,1)S(1)} %collective-permute-done.10.other, f32[384]{0:T(512)S(1)} %copy-done.1), custom_call_target="tpu_custom_call" | custom-call | flops 452984832 | bytes 2359296 | tf_op jit(solution)/shard_map/second_lead/pallas_call | solution.py:554
  24.3 0.5 %collective-permute-done.9 = bf16[6,64,256]{2,1,0:T(8,128)(2,1)S(1)} collective-permute-done((bf16[6,64,256]{2,1,0:T(8,128)(2,1)S(1)}, bf16[6,64,256]{2,1,0:T(8,128)(2,1)S(1)}, u32[]{:S(2)}, u32[]{:S(2)}) %collective-permute-start.9) | collective-permute-done | bytes 196640 | tf_op jit(solution)/shard_map/ppermute | solution.py:551
  24.8 3.2 %second_stage.1.own = bf16[2,4,64,256]{3,2,1,0:T(8,128)(2,1)S(1)} custom-call(bf16[1,6,64,256]{3,2,1,0:T(8,128)(2,1)S(1)} %bitcast.8, bf16[1,6,64,256]{3,2,1,0:T(8,128)(2,1)S(1)} %bitcast.9, bf16[3,6,64,384]{3,2,1,0:T(8,128)(2,1)S(1)} %second_lead.1.led, bf16[2,8,64,256]{3,2,1,0:T(8,128)(2,1)S(1)} %get-tuple-element.15.residual, f32[384]{0:T(512)S(1)} %copy-done.1, ...), custom_call_target="tpu_custom_call" | custom-call | tf_op jit(solution)/shard_map/second_stage/pallas_call | solution.py:563
  28.1 0.3 collective-permute-start.11
  28.4 1.3 %collective-permute-done.11.other = bf16[2,4,64,256]{3,2,1,0:T(8,128)(2,1)S(1)} collective-permute-done((bf16[2,4,64,256]{3,2,1,0:T(8,128)(2,1)S(1)}, bf16[2,4,64,256]{3,2,1,0:T(8,128)(2,1)S(1)}, u32[]{:S(2)}, u32[]{:S(2)}) %collective-permute-start.11) | collective-permute-done | bytes 262176 | tf_op jit(solution)/shard_map/ppermute | solution.py:583
  29.7 1.5 %third_stage.1 = bf16[2,4,96,128]{3,2,1,0:T(8,128)(2,1)} custom-call(bf16[2,4,64,256]{3,2,1,0:T(8,128)(2,1)S(1)} %second_stage.1.own, bf16[2,4,64,256]{3,2,1,0:T(8,128)(2,1)S(1)} %collective-permute-done.11.other, bf16[2,384,768]{2,1,0:T(8,128)(2,1)S(1)} %get-tuple-element.16.weight, f32[96]{0:T(128)S(1)} %copy-done.4), custom_call_target="tpu_custom_call" | custom-call | tf_op jit(solution)/shard_map/third_stage/pallas_call | solution.py:585
  (16 shorter events, 0.0 us)
Async XLA Ops:
  0.0 8.3 %collective-permute-start.7 = (bf16[192,432]{1,0:T(8,128)(2,1)}, bf16[192,432]{1,0:T(8,128)(2,1)S(1)}, u32[]{:S(2)}, u32[]{:S(2)}) collective-permute-start(bf16[192,432]{1,0:T(8,128)(2,1)} %bitcast.12), channel_id=1, source_target_pairs={{0,1},{1,0},{2,3},{3,2},{4,5},{5,4},{6,7},{7,6},{8,9},{9,8},{10,11... | collective-permute-start | bytes 497672 | tf_op jit(solution)/shard_map/ppermute | solution.py:497
  0.7 5.9 %collective-permute-start.2 = (bf16[4,1024]{1,0:T(4,128)(2,1)}, bf16[4,1024]{1,0:T(4,128)(2,1)S(1)}, u32[]{:S(2)}, u32[]{:S(2)}) collective-permute-start(bf16[4,1024]{1,0:T(4,128)(2,1)} %bitcast.14), channel_id=1, source_target_pairs={{0,12},{4,0},{8,4},{12,8},{1,13},{5,1},{9,5},{13,9},{2,14},{6,2},{... | collective-permute-start | bytes 24584 | tf_op jit(solution)/shard_map/ppermute | solution.py:457
  0.8 6.0 %collective-permute-start.1 = (bf16[4,1024]{1,0:T(4,128)(2,1)}, bf16[4,1024]{1,0:T(4,128)(2,1)S(1)}, u32[]{:S(2)}, u32[]{:S(2)}) collective-permute-start(bf16[4,1024]{1,0:T(4,128)(2,1)} %bitcast.15), channel_id=1, source_target_pairs={{0,8},{4,12},{8,0},{12,4},{1,9},{5,13},{9,1},{13,5},{2,10},{6,14},... | collective-permute-start | bytes 24584 | tf_op jit(solution)/shard_map/ppermute | solution.py:457
  3.2 4.9 %collective-permute-start = (bf16[4,1024]{1,0:T(4,128)(2,1)}, bf16[4,1024]{1,0:T(4,128)(2,1)S(1)}, u32[]{:S(2)}, u32[]{:S(2)}) collective-permute-start(bf16[4,1024]{1,0:T(4,128)(2,1)} %bitcast.16), channel_id=1, source_target_pairs={{0,4},{4,8},{8,12},{12,0},{1,5},{5,9},{9,13},{13,1},{2,6},{6,10},{... | collective-permute-start | bytes 24584 | tf_op jit(solution)/shard_map/ppermute | solution.py:457
  5.4 7.4 %collective-permute-start.3 = (bf16[4,1024]{1,0:T(4,128)(2,1)}, bf16[4,1024]{1,0:T(4,128)(2,1)S(1)}, u32[]{:S(2)}, u32[]{:S(2)}) collective-permute-start(bf16[4,1024]{1,0:T(4,128)(2,1)} %bitcast.17), channel_id=1, source_target_pairs={{0,2},{2,0},{1,3},{3,1},{4,6},{6,4},{5,7},{7,5},{8,10},{10,8},{9,1... | collective-permute-start | bytes 24584 | tf_op jit(solution)/shard_map/ppermute | solution.py:467
  6.6 6.2 %collective-permute-start.6 = (bf16[4,1024]{1,0:T(4,128)(2,1)S(1)}, bf16[4,1024]{1,0:T(4,128)(2,1)S(1)}, u32[]{:S(2)}, u32[]{:S(2)}) collective-permute-start(bf16[4,1024]{1,0:T(4,128)(2,1)S(1)} %collective-permute-done.2.refs_3_), channel_id=1, source_target_pairs={{0,2},{2,0},{1,3},{3,1},{4,6},{6,4},{5,7},{7,5},{8,10},{10,8},{9,1... | collective-permute-start | bytes 24584 | tf_op jit(solution)/shard_map/ppermute | solution.py:467
  6.8 6.0 %collective-permute-start.5 = (bf16[4,1024]{1,0:T(4,128)(2,1)S(1)}, bf16[4,1024]{1,0:T(4,128)(2,1)S(1)}, u32[]{:S(2)}, u32[]{:S(2)}) collective-permute-start(bf16[4,1024]{1,0:T(4,128)(2,1)S(1)} %collective-permute-done.1.refs_2_), channel_id=1, source_target_pairs={{0,2},{2,0},{1,3},{3,1},{4,6},{6,4},{5,7},{7,5},{8,10},{10,8},{9,1... | collective-permute-start | bytes 24584 | tf_op jit(solution)/shard_map/ppermute | solution.py:467
  8.0 4.8 %collective-permute-start.4 = (bf16[4,1024]{1,0:T(4,128)(2,1)S(1)}, bf16[4,1024]{1,0:T(4,128)(2,1)S(1)}, u32[]{:S(2)}, u32[]{:S(2)}) collective-permute-start(bf16[4,1024]{1,0:T(4,128)(2,1)S(1)} %collective-permute-done.refs_1_), channel_id=1, source_target_pairs={{0,2},{2,0},{1,3},{3,1},{4,6},{6,4},{5,7},{7,5},{8,10},{10,8},{9,1... | collective-permute-start | bytes 24584 | tf_op jit(solution)/shard_map/ppermute | solution.py:467
  8.3 4.5 %collective-permute-start.8 = (f32[192]{0:T(256)}, f32[192]{0:T(256)S(1)}, u32[]{:S(2)}, u32[]{:S(2)}) collective-permute-start(f32[192]{0:T(256)} %refs_11_.1), channel_id=1, source_target_pairs={{0,1},{1,0},{2,3},{3,2},{4,5},{5,4},{6,7},{7,6},{8,9},{9,8},{10,11... | collective-permute-start | bytes 2312 | tf_op jit(solution)/shard_map/ppermute | solution.py:473
  10.3 10.6 %copy-start.2 = (f32[192]{0:T(256)S(1)}, f32[192]{0:T(256)}, u32[]{:S(2)}) copy-start(f32[192]{0:T(256)} %conv_bias.2) | copy-start | bytes 2308
  20.2 3.4 %copy-start.1 = (f32[384]{0:T(512)S(1)}, f32[384]{0:T(512)}, u32[]{:S(2)}) copy-start(f32[384]{0:T(512)} %gain.3) | copy-start | bytes 4612
  20.2 3.4 %collective-permute-start.10 = (bf16[3,6,64,256]{3,2,1,0:T(8,128)(2,1)S(1)}, bf16[3,6,64,256]{3,2,1,0:T(8,128)(2,1)S(1)}, u32[]{:S(2)}, u32[]{:S(2)}) collective-permute-start(bf16[3,6,64,256]{3,2,1,0:T(8,128)(2,1)S(1)} %get-tuple-element.14.own), channel_id=1, source_target_pairs={{0,1},{1,0},{2,3},{3,2},{4,5},{5,4},{6,7},{7,6},{8,9},{9,8},{10,11... | collective-permute-start | bytes 1769480 | tf_op jit(solution)/shard_map/ppermute | solution.py:540
  20.9 4.0 %copy-start = (bf16[9,1152,192]{1,2,0:T(8,128)(2,1)S(1)}, bf16[9,1152,192]{1,2,0:T(8,128)(2,1)}, u32[]{:S(2)}) copy-start(bf16[9,1152,192]{1,2,0:T(8,128)(2,1)} %param.18) | copy-start | bytes 11943940
  20.9 4.0 %copy-start.3 = (f32[192]{0:T(256)S(1)}, f32[192]{0:T(256)}, u32[]{:S(2)}) copy-start(f32[192]{0:T(256)} %conv_bias.3) | copy-start | bytes 2308
  23.3 6.3 %copy-start.4 = (f32[96]{0:T(128)S(1)}, f32[96]{0:T(128)}, u32[]{:S(2)}) copy-start(f32[96]{0:T(128)} %up_bias.1) | copy-start | bytes 1156
  23.3 1.5 %collective-permute-start.9 = (bf16[6,64,256]{2,1,0:T(8,128)(2,1)S(1)}, bf16[6,64,256]{2,1,0:T(8,128)(2,1)S(1)}, u32[]{:S(2)}, u32[]{:S(2)}) collective-permute-start(bf16[6,64,256]{2,1,0:T(8,128)(2,1)S(1)} %first_last.1), channel_id=1, source_target_pairs={{0,1},{1,0},{2,3},{3,2},{4,5},{5,4},{6,7},{7,6},{8,9},{9,8},{10,11... | collective-permute-start | bytes 589832 | tf_op jit(solution)/shard_map/ppermute | solution.py:551
  28.1 1.6 %collective-permute-start.11 = (bf16[2,4,64,256]{3,2,1,0:T(8,128)(2,1)S(1)}, bf16[2,4,64,256]{3,2,1,0:T(8,128)(2,1)S(1)}, u32[]{:S(2)}, u32[]{:S(2)}) collective-permute-start(bf16[2,4,64,256]{3,2,1,0:T(8,128)(2,1)S(1)} %second_stage.1.own), channel_id=1, source_target_pairs={{0,1},{1,0},{2,3},{3,2},{4,5},{5,4},{6,7},{7,6},{8,9},{9,8},{10,11... | collective-permute-start | bytes 786440 | tf_op jit(solution)/shard_map/ppermute | solution.py:583
